TPU v7x, 1024 devices: a whole 4x8x16 slice. The times are simulated.
1024 devices in a mesh: elem: 128 (over y, z), lev: 8 (over x, core).
Axes of the slice: x: 4, y: 8, z: 16, core: 2. Of those that a mesh axis runs over, the one named last changes fastest.
Arguments:
- tracers: bfloat16 [16384, 32, 1024], P('elem', 'lev'), may hold values from -6 to 6
- velocity: float32 [3, 16, 32, 16384], P(None, None, 'lev', 'elem'), may hold values from -6 to 6
- node_mass: float32 [16, 16384], P(None, 'elem'), may hold values from 0.5 to 2
- source: int32 [16384], P('elem'), may hold values from 0 to 16383, as said below
Outputs:
- advected: bfloat16 [16384, 32, 1024], P('elem', 'lev')
Inputs may be any that keep to these rules, and one draw needn't show every extreme that they name: The source of element e lies at most 64 elements before or after e along the curve, cyclically over 16384 elements. Within each aligned run of 128 elements, only the first 32 may take a source before the run and only the last 32 one after it; in every draw some run has all of its first 32 elements taking sources 64 elements before them, and some run all of its last 32 elements taking sources 64 elements after them.
All inputs are finite; a program needn't handle non-finite values.
Results may differ from a plain program's by a relative error of at most 0.006.
Values may be sent and summed in bfloat16 or wider, within the bound.
A program may use at most 32 MiB of HBM per device.

v0:
```python
import jax
import jax.numpy as jnp
import numpy as np
from jax import lax
from jax.sharding import PartitionSpec as P

gll_points = (-1.0, -0.4472135954999579, 0.4472135954999579, 1.0)
east_nodes = np.array([3, 7, 11, 15])
west_nodes = np.array([0, 4, 8, 12])
courant = 0.15


def passed_along(value, axis, steps):
    count = lax.axis_size(axis)
    first, last = (max(0, -steps), min(count, count - steps))
    return lax.ppermute(value, axis, [(source, source + steps) for source in range(first, last)])


def from_behind(array, axis, by):
    peers = lax.axis_size(axis)
    return lax.ppermute(array, axis, [(i, (i + by) % peers) for i in range(peers)])


def with_halo(cells, sides, width):
    for axis, dim in sides:
        count = lax.axis_size(axis)
        head = lax.slice_in_dim(cells, 0, width, axis=dim)
        tail = lax.slice_in_dim(cells, cells.shape[dim] - width, cells.shape[dim], axis=dim)
        cells = jnp.concatenate(
            [
                lax.ppermute(tail, axis, [(i, (i + 1) % count) for i in range(count)]),
                cells,
                lax.ppermute(head, axis, [((i + 1) % count, i) for i in range(count)]),
            ],
            axis=dim,
        )
    return cells


def lagrange(position):
    columns = []
    for column in range(4):
        factor = jnp.ones_like(position)
        for other in range(4):
            if other != column:
                factor = (
                    factor
                    * (position - gll_points[other])
                    / (gll_points[column] - gll_points[other])
                )
        columns.append(factor)
    return jnp.stack(columns, axis=0)


def weights(horizontal):
    along_nodes = jnp.array([gll_points[node % 4] for node in range(16)], jnp.float32)[
        :, None, None
    ]
    across_nodes = jnp.array([gll_points[node // 4] for node in range(16)], jnp.float32)[
        :, None, None
    ]
    along_basis = lagrange(along_nodes - courant * horizontal[0])
    across_basis = lagrange(across_nodes - courant * horizontal[1])
    table = across_basis[:, None] * along_basis[None, :]
    return table.reshape((16,) + table.shape[2:]).astype(jnp.bfloat16)


def share_wind(field, mass_east, mass_west, prev_east, prev_mass, next_west, next_mass):
    east = field[:, east_nodes]
    west = field[:, west_nodes]
    west_after = jnp.concatenate([west[..., 1:], next_west], axis=-1)
    mass_after = jnp.concatenate([mass_west[..., 1:], next_mass], axis=-1)
    shared = (mass_east * east + mass_after * west_after) / (mass_east + mass_after)
    east_before = jnp.concatenate([prev_east, east[..., :-1]], axis=-1)
    mass_before = jnp.concatenate([prev_mass, mass_east[..., :-1]], axis=-1)
    shared_west = (mass_before * east_before + mass_west * west) / (mass_before + mass_west)
    field = field.at[:, east_nodes].set(shared)
    return field.at[:, west_nodes].set(shared_west)


def share_columns(field, width, mass_east, mass_west, prev_east, prev_mass, next_west, next_mass):
    east = field[..., 3 * width :]
    west = field[..., :width]
    west_after = jnp.concatenate([west[1:], next_west], axis=0)
    mass_after = jnp.concatenate([mass_west[1:], next_mass], axis=0)
    shared = (mass_east * east + mass_after * west_after) / (mass_east + mass_after)
    east_before = jnp.concatenate([prev_east, east[:-1]], axis=0)
    mass_before = jnp.concatenate([prev_mass, mass_east[:-1]], axis=0)
    shared_west = (mass_before * east_before + mass_west * west) / (mass_before + mass_west)
    return jnp.concatenate([shared_west, field[..., width : 3 * width], shared], axis=-1)


def on_device(tracers, velocity, node_mass, source):
    elements, levels_here, columns_all = tracers.shape
    tracer_count = columns_all // 16
    total = elements * lax.axis_size("elem")
    start = lax.axis_index("elem") * elements
    shape_four = (elements, levels_here, 16, tracer_count)
    top_row = passed_along(tracers[:, levels_here - 1 :, :], "lev", 1)
    upper = jnp.concatenate([top_row, tracers[:, : levels_here - 1, :]], axis=1)
    descent = jnp.transpose(jax.nn.sigmoid(velocity[2]), (2, 1, 0))[..., None]
    descent_wide = jnp.broadcast_to(descent, shape_four).reshape(elements, levels_here, columns_all)
    lifted = (
        (1.0 - descent_wide) * tracers.astype(jnp.float32)
        + descent_wide * upper.astype(jnp.float32)
    ).astype(jnp.bfloat16)
    horizontal = velocity[:2]
    mass_east = node_mass[east_nodes]
    mass_west = node_mass[west_nodes]
    mass_east_wide = jnp.broadcast_to(mass_east[None, :, None, :], (1, 4, levels_here, elements))
    mass_west_wide = jnp.broadcast_to(mass_west[None, :, None, :], (1, 4, levels_here, elements))
    east_pack = jnp.concatenate(
        [horizontal[:, east_nodes, :, elements - 1 :], mass_east_wide[..., elements - 1 :]], axis=0
    )
    west_pack = jnp.concatenate([horizontal[:, west_nodes, :, :1], mass_west_wide[..., :1]], axis=0)
    wind_received = []
    for offset, packed in ((1, east_pack), (-1, west_pack)):
        wind_received.append(from_behind(packed, "elem", offset))
    prev_pack, next_pack = wind_received
    horizontal = share_wind(
        horizontal,
        mass_east_wide,
        mass_west_wide,
        prev_pack[:2],
        prev_pack[2:3],
        next_pack[:2],
        next_pack[2:3],
    )
    table = weights(horizontal)
    relative = (source - start) % total
    span = elements // 2
    padded = with_halo(lifted, (("elem", 0),), span)
    blocks = jnp.take(padded, (relative + span) % total, axis=0)
    moved = jnp.einsum(
        "mnke,ekmt->eknt", table, blocks.reshape(shape_four), preferred_element_type=jnp.float32
    ).astype(jnp.bfloat16)
    moved = moved.reshape(elements, levels_here, 4, 4 * tracer_count)
    east_last = moved[elements - 1 :, :, :, 3 * tracer_count :]
    west_first = moved[:1, :, :, :tracer_count]
    edge_received = []
    for offset, packed in ((1, east_last), (-1, west_first)):
        edge_received.append(from_behind(packed, "elem", offset))
    mass_east_rows = jnp.transpose(mass_east)[:, None, :, None]
    mass_west_rows = jnp.transpose(mass_west)[:, None, :, None]
    prev_mass_rows = prev_pack[2, :, 0, 0].reshape(1, 1, 4, 1)
    next_mass_rows = next_pack[2, :, 0, 0].reshape(1, 1, 4, 1)
    final = share_columns(
        moved.astype(jnp.float32),
        tracer_count,
        mass_east_rows,
        mass_west_rows,
        edge_received[0].astype(jnp.float32),
        prev_mass_rows,
        edge_received[1].astype(jnp.float32),
        next_mass_rows,
    )
    return final.astype(jnp.bfloat16).reshape(elements, levels_here, columns_all)


def solution(mesh):
    placed = (P("elem", "lev", None), P(None, None, "lev", "elem"), P(None, "elem"), P("elem"))
    return jax.shard_map(
        on_device, mesh=mesh, in_specs=placed, out_specs=P("elem", "lev", None), check_vma=False
    )
```

profile of v0, /device:TPU:2, one launch (start us, length us, event | category | flops | bytes accessed | tf_op | source)
XLA Modules:
  0.0 109.9 jit_solution(15687925485360189149)
XLA Ops:
  0.0 2.6 %slice.123 = bf16[128,1,1024]{2,1,0:T(2,128)(2,1)} slice(bf16[128,4,1024]{2,1,0:T(4,128)(2,1)} %param.16), slice={[0:128], [3:4], [0:1024]} | slice | bytes 524288 | tf_op jit(solution)/shard_map/slice | solution.py:99
  2.7 1.9 %collective-permute-start.2 = (bf16[128,1,1024]{2,1,0:T(2,128)(2,1)}, bf16[128,1,1024]{2,1,0:T(2,128)(2,1)}, u32[]{:S(2)}, u32[]{:S(2)}) collective-permute-start(bf16[128,1,1024]{2,1,0:T(2,128)(2,1)} %slice.123), channel_id=1, source_target_pairs={{0,1},{1,2},{2,3},{3,4},{4,5},{5,6},{6,7},{8,9},{9,10},{10,11},{11... | collective-permute-start | bytes 786440 | tf_op jit(solution)/shard_map/ppermute | solution.py:16
  4.6 0.7 pad_clamp_fusion.2
  6.0 0.8 slice.104
  6.8 1.1 %copy.170 = f32[2,16,4,128]{2,0,3,1:T(2,128)S(1)} copy(f32[2,16,4,128]{3,2,1,0:T(4,128)S(1)} %slice.104) | data formatting | bytes 131072
  8.6 4.3 %collective-permute-start = (f32[3,4,4,1]{2,1,0,3:T(4,128)S(1)}, f32[3,4,4,1]{2,1,0,3:T(4,128)S(1)}, u32[]{:S(2)}, u32[]{:S(2)}) collective-permute-start(f32[3,4,4,1]{2,1,0,3:T(4,128)S(1)} %pad_maximum_fusion.4), channel_id=1, source_target_pairs={{0,8},{8,16},{16,24},{24,32},{32,40},{40,48},{48,56},{56,64},{64,7... | collective-permute-start | bytes 584 | tf_op jit(solution)/shard_map/ppermute | solution.py:21
  14.3 18.8 %collective-permute-start.1 = (f32[3,4,4,1]{2,1,0,3:T(4,128)S(1)}, f32[3,4,4,1]{2,1,0,3:T(4,128)S(1)}, u32[]{:S(2)}, u32[]{:S(2)}) collective-permute-start(f32[3,4,4,1]{2,1,0,3:T(4,128)S(1)} %pad_maximum_fusion.5), channel_id=1, source_target_pairs={{0,1016},{8,0},{16,8},{24,16},{32,24},{40,32},{48,40},{56,48},{64,... | collective-permute-start | bytes 584 | tf_op jit(solution)/shard_map/ppermute | solution.py:21
  33.1 1.1 %gather_fusion.5 = f32[4,2,4,128]{2,1,3,0:T(2,128)S(1)} fusion(f32[2,16,4,128]{2,0,3,1:T(2,128)S(1)} %copy.170, s32[1024]{0:T(1024)S(1)} %pad_clamp_fusion.1), kind=kCustom, calls=%fused_computation.5 | custom fusion | bytes 32784 | tf_op jit(solution)/shard_map/gather | solution.py:70
  34.3 1.1 %gather_fusion.2 = f32[4,2,4,128]{2,1,3,0:T(2,128)S(1)} fusion(f32[2,16,4,128]{2,0,3,1:T(2,128)S(1)} %copy.170, s32[1024]{0:T(1024)S(1)} %pad_clamp_fusion.2), kind=kCustom, calls=%fused_computation.2 | custom fusion | bytes 32784 | tf_op jit(solution)/shard_map/gather | solution.py:69
  35.7 2.1 %copy.160 = f32[128,4,1024]{2,1,0:T(4,128)} copy(f32[128,4,1024]{0,2,1:T(8,128)S(1)} %bitcast.62) | data formatting | bytes 4194304 | tf_op jit(solution)/shard_map/reshape | solution.py:102
  37.7 0.6 broadcast_multiply_fusion
  38.6 0.6 broadcast_multiply_fusion.1
  41.4 0.7 scatter_fusion
  42.9 0.7 scatter_fusion.1
  43.9 3.0 %copy.163 = bf16[16,16,4,128]{0,1,2,3:T(8,128)(2,1)S(1)} copy(bf16[16,16,4,128]{3,1,2,0:T(8,128)(2,1)S(1)} %bitcast.70) | data formatting | bytes 524288 | tf_op jit(solution)/shard_map/convert_element_type | solution.py:65
  46.9 3.5 %add_convert_fusion = bf16[128,4,1024]{2,1,0:T(4,128)(2,1)S(1)} fusion(f32[128,4,1024]{2,1,0:T(4,128)} %copy.160, bf16[128,4,1024]{2,1,0:T(4,128)(2,1)S(1)} %copy-done.1, bf16[128,3,1024]{2,1,0:T(4,128)(2,1)S(1)} %bitcast.63, bf16[128,1,1024]{2,1,0:T(2,128)(2,1)} %collective-permute-done.2), kind=kLoop, calls=%fused_computation.10 | loop fusion | flops 5242880 | bytes 5242880 | tf_op jit(solution)/shard_map/convert_element_type | solution.py:106
  50.8 1.9 %collective-permute-start.3 = (bf16[64,4,1024]{2,1,0:T(4,128)(2,1)S(1)}, bf16[64,4,1024]{2,1,0:T(4,128)(2,1)S(1)}, u32[]{:S(2)}, u32[]{:S(2)}) collective-permute-start(bf16[64,4,1024]{2,1,0:T(4,128)(2,1)S(1)} %get-tuple-element.13), channel_id=1, source_target_pairs={{0,8},{8,16},{16,24},{24,32},{32,40},{40,48},{48,56},{56,64},{64,7... | collective-permute-start | bytes 1572872 | tf_op jit(solution)/shard_map/ppermute | solution.py:31
  52.7 7.4 %collective-permute-start.4 = (bf16[64,4,1024]{2,1,0:T(4,128)(2,1)S(1)}, bf16[64,4,1024]{2,1,0:T(4,128)(2,1)S(1)}, u32[]{:S(2)}, u32[]{:S(2)}) collective-permute-start(bf16[64,4,1024]{2,1,0:T(4,128)(2,1)S(1)} %get-tuple-element.14), channel_id=1, source_target_pairs={{8,0},{16,8},{24,16},{32,24},{40,32},{48,40},{56,48},{64,56},{72,6... | collective-permute-start | bytes 1572872 | tf_op jit(solution)/shard_map/ppermute | solution.py:33
  60.3 10.1 %collective-permute-done.3 = bf16[64,4,1024]{2,1,0:T(4,128)(2,1)S(1)} collective-permute-done((bf16[64,4,1024]{2,1,0:T(4,128)(2,1)S(1)}, bf16[64,4,1024]{2,1,0:T(4,128)(2,1)S(1)}, u32[]{:S(2)}, u32[]{:S(2)}) %collective-permute-start.3) | collective-permute-done | bytes 524320 | tf_op jit(solution)/shard_map/ppermute | solution.py:31
  70.5 1.7 %collective-permute-done.4 = bf16[64,4,1024]{2,1,0:T(4,128)(2,1)S(1)} collective-permute-done((bf16[64,4,1024]{2,1,0:T(4,128)(2,1)S(1)}, bf16[64,4,1024]{2,1,0:T(4,128)(2,1)S(1)}, u32[]{:S(2)}, u32[]{:S(2)}) %collective-permute-start.4) | collective-permute-done | bytes 524320 | tf_op jit(solution)/shard_map/ppermute | solution.py:33
  72.2 2.5 %pad_maximum_fusion = bf16[256,4,1024]{2,1,0:T(4,128)(2,1)} fusion(bf16[64,4,1024]{2,1,0:T(4,128)(2,1)S(1)} %collective-permute-done.4, bf16[128,4,1024]{2,1,0:T(4,128)(2,1)S(1)} %add_convert_fusion, bf16[64,4,1024]{2,1,0:T(4,128)(2,1)S(1)} %collective-permute-done.3), kind=kLoop, calls=%fused_computation.9 | loop fusion | flops 2097152 | bytes 4194304 | tf_op jit(solution)/shard_map/concatenate | solution.py:29
  74.7 3.0 %gather_fusion.6 = bf16[128,4,1024]{2,1,0:T(4,128)(2,1)S(1)} fusion(bf16[256,4,1024]{2,1,0:T(4,128)(2,1)} %pad_maximum_fusion, s32[1024]{0:T(1024)S(1)} %pad_clamp_fusion), kind=kCustom, calls=%fused_computation.6 | custom fusion | bytes 2097664 | tf_op jit(solution)/shard_map/jit(_take)/gather | solution.py:133
  77.7 1.7 %copy.162 = bf16[128,4,1024]{0,2,1:T(8,128)(2,1)} copy(bf16[128,4,1024]{2,1,0:T(4,128)(2,1)S(1)} %gather_fusion.6) | data formatting | bytes 2097152 | tf_op jit(solution)/shard_map/jit(_take)/gather | solution.py:133
  79.4 1.3 %broadcast_select_fusion = bf16[128,4,16,64]{0,3,2,1:T(8,128)(2,1)S(1)} fusion(bf16[128,4,16,64]{0,3,2,1:T(8,128)(2,1)} %bitcast.64, pred[128]{0:T(512)(128)(4,1)S(1)} %get-tuple-element.5), kind=kLoop, calls=%fused_computation.13 | loop fusion | flops 524288 | bytes 2097280 | tf_op jit(solution)/shard_map/jit(_take)/select_n | solution.py:133
  80.7 3.8 %copy.164 = bf16[128,4,16,64]{3,2,1,0:T(8,128)(2,1)} copy(bf16[128,4,16,64]{0,3,2,1:T(8,128)(2,1)S(1)} %broadcast_select_fusion) | data formatting | bytes 2097152 | tf_op jit(solution)/shard_map/jit(_take)/select_n | solution.py:133
  84.5 4.1 %convolution_convert_fusion = bf16[128,4,16,64]{3,2,1,0:T(8,128)(2,1)} fusion(bf16[16,16,4,128]{0,1,2,3:T(8,128)(2,1)S(1)} %copy.163, bf16[128,4,16,64]{3,2,1,0:T(8,128)(2,1)} %copy.164), kind=kOutput, calls=%fused_computation.11 | convolution fusion | flops 17301504 | bytes 2359296 | tf_op jit(solution)/shard_map/mnke,ekmt->eknt/dot_general | solution.py:134
  88.7 3.3 %copy.165 = bf16[128,4,16,64]{0,3,2,1:T(8,128)(2,1)S(1)} copy(bf16[128,4,16,64]{3,2,1,0:T(8,128)(2,1)} %convolution_convert_fusion) | data formatting | bytes 2097152 | tf_op jit(solution)/shard_map/convert_element_type | solution.py:136
  92.1 1.9 %collective-permute-start.5 = (bf16[1,4,4,64]{0,3,2,1:T(8,128)(2,1)S(1)}, bf16[1,4,4,64]{0,3,2,1:T(8,128)(2,1)S(1)}, u32[]{:S(2)}, u32[]{:S(2)}) collective-permute-start(bf16[1,4,4,64]{0,3,2,1:T(8,128)(2,1)S(1)} %get-tuple-element.11), channel_id=1, source_target_pairs={{0,8},{8,16},{16,24},{24,32},{32,40},{40,48},{48,56},{56,64},{64,7... | collective-permute-start | bytes 6152 | tf_op jit(solution)/shard_map/ppermute | solution.py:21
  94.1 7.7 %collective-permute-start.6 = (bf16[1,4,4,64]{0,3,2,1:T(8,128)(2,1)S(1)}, bf16[1,4,4,64]{0,3,2,1:T(8,128)(2,1)S(1)}, u32[]{:S(2)}, u32[]{:S(2)}) collective-permute-start(bf16[1,4,4,64]{0,3,2,1:T(8,128)(2,1)S(1)} %get-tuple-element.12), channel_id=1, source_target_pairs={{0,1016},{8,0},{16,8},{24,16},{32,24},{40,32},{48,40},{56,48},{64,... | collective-permute-start | bytes 6152 | tf_op jit(solution)/shard_map/ppermute | solution.py:21
  102.2 4.2 %collective-permute-done.5 = bf16[1,4,4,64]{0,3,2,1:T(8,128)(2,1)S(1)} collective-permute-done((bf16[1,4,4,64]{0,3,2,1:T(8,128)(2,1)S(1)}, bf16[1,4,4,64]{0,3,2,1:T(8,128)(2,1)S(1)}, u32[]{:S(2)}, u32[]{:S(2)}) %collective-permute-start.5) | collective-permute-done | bytes 2080 | tf_op jit(solution)/shard_map/ppermute | solution.py:21
  106.5 1.1 %collective-permute-done.6 = bf16[1,4,4,64]{0,3,2,1:T(8,128)(2,1)S(1)} collective-permute-done((bf16[1,4,4,64]{0,3,2,1:T(8,128)(2,1)S(1)}, bf16[1,4,4,64]{0,3,2,1:T(8,128)(2,1)S(1)}, u32[]{:S(2)}, u32[]{:S(2)}) %collective-permute-start.6) | collective-permute-done | bytes 2080 | tf_op jit(solution)/shard_map/ppermute | solution.py:21
  108.2 1.7 %copy.169 = bf16[128,4,1024]{2,1,0:T(4,128)(2,1)} copy(bf16[128,4,1024]{0,2,1:T(8,128)(2,1)S(1)} %bitcast.65) | data formatting | bytes 2097152 | tf_op jit(solution)/shard_map/convert_element_type | solution.py:157
  (89 shorter events, 8.1 us)
Async XLA Ops:
  0.0 5.2 %copy-start = (f32[16,128]{1,0:T(8,128)S(1)}, f32[16,128]{1,0:T(8,128)}, u32[]{:S(2)}) copy-start(f32[16,128]{1,0:T(8,128)} %param.18) | copy-start | bytes 24580
  0.0 8.0 %copy-start.2 = (s32[4]{0:T(128)S(1)}, s32[4]{0:T(128)}, u32[]{:S(2)}) copy-start(s32[4]{0:T(128)} %constant.166) | copy-start | bytes 52
  0.0 35.5 %slice-start = ((f32[3,16,4,128]{3,2,1,0:T(4,128)}), f32[1,16,4,128]{3,2,1,0:T(4,128)S(1)}, s32[]{:S(2)}) async-start(f32[3,16,4,128]{3,2,1,0:T(4,128)} %param.17), calls=%async_computation | async-start | bytes 65536 | tf_op jit(solution)/shard_map/slice | solution.py:101
  0.0 35.4 %copy-start.6 = (s32[128]{0:T(128)S(1)}, s32[128]{0:T(128)}, u32[]{:S(2)}) copy-start(s32[128]{0:T(128)} %param.19) | copy-start | bytes 1540
  2.7 44.3 %collective-permute-start.2 = (bf16[128,1,1024]{2,1,0:T(2,128)(2,1)}, bf16[128,1,1024]{2,1,0:T(2,128)(2,1)}, u32[]{:S(2)}, u32[]{:S(2)}) collective-permute-start(bf16[128,1,1024]{2,1,0:T(2,128)(2,1)} %slice.123), channel_id=1, source_target_pairs={{0,1},{1,2},{2,3},{3,4},{4,5},{5,6},{6,7},{8,9},{9,10},{10,11},{11... | collective-permute-start | bytes 786440 | tf_op jit(solution)/shard_map/ppermute | solution.py:16
  8.6 31.3 %collective-permute-start = (f32[3,4,4,1]{2,1,0,3:T(4,128)S(1)}, f32[3,4,4,1]{2,1,0,3:T(4,128)S(1)}, u32[]{:S(2)}, u32[]{:S(2)}) collective-permute-start(f32[3,4,4,1]{2,1,0,3:T(4,128)S(1)} %pad_maximum_fusion.4), channel_id=1, source_target_pairs={{0,8},{8,16},{16,24},{24,32},{32,40},{40,48},{48,56},{56,64},{64,7... | collective-permute-start | bytes 584 | tf_op jit(solution)/shard_map/ppermute | solution.py:21
  14.3 26.0 %collective-permute-start.1 = (f32[3,4,4,1]{2,1,0,3:T(4,128)S(1)}, f32[3,4,4,1]{2,1,0,3:T(4,128)S(1)}, u32[]{:S(2)}, u32[]{:S(2)}) collective-permute-start(f32[3,4,4,1]{2,1,0,3:T(4,128)S(1)} %pad_maximum_fusion.5), channel_id=1, source_target_pairs={{0,1016},{8,0},{16,8},{24,16},{32,24},{40,32},{48,40},{56,48},{64,... | collective-permute-start | bytes 584 | tf_op jit(solution)/shard_map/ppermute | solution.py:21
  39.2 2.2 %copy-start.3 = (s32[4]{0:T(128)S(1)}, s32[4]{0:T(128)}, u32[]{:S(2)}) copy-start(s32[4]{0:T(128)} %constant.167) | copy-start | bytes 52
  39.3 4.3 %copy-start.4 = (f32[16]{0:T(128)S(1)}, f32[16]{0:T(128)}, u32[]{:S(2)}) copy-start(f32[16]{0:T(128)} %constant.124.clone) | copy-start | bytes 196
  39.3 4.3 %copy-start.5 = (f32[16]{0:T(128)S(1)}, f32[16]{0:T(128)}, u32[]{:S(2)}) copy-start(f32[16]{0:T(128)} %constant.123.clone) | copy-start | bytes 196
  42.9 4.0 %copy-start.1 = (bf16[128,4,1024]{2,1,0:T(4,128)(2,1)S(1)}, bf16[128,4,1024]{2,1,0:T(4,128)(2,1)}, u32[]{:S(2)}) copy-start(bf16[128,4,1024]{2,1,0:T(4,128)(2,1)} %param.16) | copy-start | bytes 3145732
  50.8 19.7 %collective-permute-start.3 = (bf16[64,4,1024]{2,1,0:T(4,128)(2,1)S(1)}, bf16[64,4,1024]{2,1,0:T(4,128)(2,1)S(1)}, u32[]{:S(2)}, u32[]{:S(2)}) collective-permute-start(bf16[64,4,1024]{2,1,0:T(4,128)(2,1)S(1)} %get-tuple-element.13), channel_id=1, source_target_pairs={{0,8},{8,16},{16,24},{24,32},{32,40},{40,48},{48,56},{56,64},{64,7... | collective-permute-start | bytes 1572872 | tf_op jit(solution)/shard_map/ppermute | solution.py:31
  52.7 19.5 %collective-permute-start.4 = (bf16[64,4,1024]{2,1,0:T(4,128)(2,1)S(1)}, bf16[64,4,1024]{2,1,0:T(4,128)(2,1)S(1)}, u32[]{:S(2)}, u32[]{:S(2)}) collective-permute-start(bf16[64,4,1024]{2,1,0:T(4,128)(2,1)S(1)} %get-tuple-element.14), channel_id=1, source_target_pairs={{8,0},{16,8},{24,16},{32,24},{40,32},{48,40},{56,48},{64,56},{72,6... | collective-permute-start | bytes 1572872 | tf_op jit(solution)/shard_map/ppermute | solution.py:33
  92.1 14.3 %collective-permute-start.5 = (bf16[1,4,4,64]{0,3,2,1:T(8,128)(2,1)S(1)}, bf16[1,4,4,64]{0,3,2,1:T(8,128)(2,1)S(1)}, u32[]{:S(2)}, u32[]{:S(2)}) collective-permute-start(bf16[1,4,4,64]{0,3,2,1:T(8,128)(2,1)S(1)} %get-tuple-element.11), channel_id=1, source_target_pairs={{0,8},{8,16},{16,24},{24,32},{32,40},{40,48},{48,56},{56,64},{64,7... | collective-permute-start | bytes 6152 | tf_op jit(solution)/shard_map/ppermute | solution.py:21
  94.1 13.5 %collective-permute-start.6 = (bf16[1,4,4,64]{0,3,2,1:T(8,128)(2,1)S(1)}, bf16[1,4,4,64]{0,3,2,1:T(8,128)(2,1)S(1)}, u32[]{:S(2)}, u32[]{:S(2)}) collective-permute-start(bf16[1,4,4,64]{0,3,2,1:T(8,128)(2,1)S(1)} %get-tuple-element.12), channel_id=1, source_target_pairs={{0,1016},{8,0},{16,8},{24,16},{32,24},{40,32},{48,40},{56,48},{64,... | collective-permute-start | bytes 6152 | tf_op jit(solution)/shard_map/ppermute | solution.py:21
where the time goes:
time: 110 us
  starting transfers between devices  43.9 us (40%)
  local copies, waits for them, and re-layouts  33.3 us (30%)
  waiting for transfers between devices  17.2 us (16%)
  other arithmetic  10.9 us (10%)
  matrix products  4.13 us (4%)
    ppermute x4, starting transfers between devices, from_behind(): lax.ppermute(array, axis, [(i, (i + by) % peers) for i in range(peers)])  32.7 us
    ppermute x1, waiting for transfers between devices, with_halo(): lax.ppermute(tail, axis, [(i, (i + 1) % count) for i in range(count)])  10.1 us
    ppermute x1, starting transfers between devices, with_halo(): lax.ppermute(head, axis, [((i + 1) % count, i) for i in range(count)])  7.42 us
    ppermute x4, waiting for transfers between devices, from_behind(): lax.ppermute(array, axis, [(i, (i + by) % peers) for i in range(peers)])  5.32 us
    gather x2, local copies, waits for them, and re-layouts, on_device(): blocks = jnp.take(padded, (relative + span) % total, axis=0)  4.74 us
    dot_general x1, matrix products, on_device(): jnp.einsum('mnke,ekmt->eknt', table, blocks.reshape(shape_four), preferre...  4.13 us
    select_n x1, local copies, waits for them, and re-layouts, on_device(): blocks = jnp.take(padded, (relative + span) % total, axis=0)  3.79 us
    convert_element_type x1, other arithmetic, on_device(): lifted = ((1.0 - descent_wide) * tracers.astype(jnp.float32) + descent_wi...  3.49 us
  transfers between devices with their start and end apart: 7, of which 4 were waited for; matrix products, arithmetic and copies ran while one was open for 18% of the time, Pallas kernels for 0%

commit v1 on v0

v1 whole, which is shorter than its diff:
```python
import functools

import jax
import jax.numpy as jnp
from jax import lax
from jax.experimental import pallas as pl
from jax.experimental.pallas import tpu as pltpu
from jax.sharding import PartitionSpec as P

MESH = pl.DeviceIdType.MESH
gll = (-1.0, -0.4472135954999579, 0.4472135954999579, 1.0)
courant = 0.15
f32 = jnp.float32
bf16 = jnp.bfloat16
CH = 4
TQ = 64 // CH


def dot(a, b):
    return lax.dot_general(a, b, (((1,), (0,)), ((), ())), preferred_element_type=f32)


def dot_t(a, b):
    return lax.dot_general(a, b, (((1,), (1,)), ((), ())), preferred_element_type=f32)


def dot_exact(a, b):
    return lax.dot_general(
        a, b, (((1,), (0,)), ((), ())), preferred_element_type=f32, precision=lax.Precision.HIGHEST
    )


def iota(shape, dim):
    return lax.broadcasted_iota(jnp.int32, shape, dim)


def one_hot(rows, code):
    return jnp.where(iota((rows, code.shape[1]), 0) == code, 1.0, 0.0).astype(bf16)


def basis(x):
    out = []
    for a in range(4):
        others = [b for b in range(4) if b != a]
        scale = 1.0
        for b in others:
            scale = scale / (gll[a] - gll[b])
        f = (x - gll[others[0]]) * (x - gll[others[1]]) * (x - gll[others[2]]) * scale
        out.append(f)
    return out


def kernel(
    peers_elem, peers_lev, total,
    t_ref, v_ref, mass_ref, src_ref, o_ref,
    tt, wind, massx, msg_to_next, msg_to_prev, msg_prev, msg_next,
    x3_send, x3_recv, lifted, pack_next, pack_prev, halo_prev, halo_next,
    gath, wtab, moved, edge_to_next, edge_to_prev, edges,
    msg_sem, x3_sem, halo_sem, edge_sem,
):
    elem = lax.axis_index("elem")
    lev = lax.axis_index("lev")
    nxt = lax.rem(elem + 1, peers_elem)
    prv = lax.rem(elem + peers_elem - 1, peers_elem)
    below = lax.rem(lev + 1, peers_lev)
    above = lax.rem(lev + peers_lev - 1, peers_lev)

    barrier = pltpu.get_barrier_semaphore()
    for target in ({"elem": nxt}, {"elem": prv}, {"lev": below}, {"lev": above}):
        pl.semaphore_signal(barrier, inc=1, device_id=target, device_id_type=MESH)

    def remote(src, dst, sems, target):
        return pltpu.make_async_remote_copy(
            src_ref=src, dst_ref=dst, send_sem=sems.at[0], recv_sem=sems.at[1],
            device_id=target, device_id_type=MESH,
        )

    lane = iota((1, 128), 1)
    level = jnp.bitwise_and(lane, 3)
    wide_lane = iota((128, 512), 1)
    wide_row = iota((128, 512), 0)

    mass_all = mass_ref[...]
    start = elem * 128
    rel = src_ref[...] - start + 64
    rel = jnp.where(rel < 0, rel + total, rel)
    rel = jnp.where(rel >= total, rel - total, rel)
    rel8 = jnp.broadcast_to(rel.astype(f32), (8, 128))
    spread_all = jnp.where(wide_row == jnp.right_shift(wide_lane, 2), 1.0, 0.0)
    mass_wide = dot_exact(mass_all, spread_all)
    rel_wide = dot_exact(rel8, spread_all)
    acc = None
    for k in range(4):
        spread = jnp.where(wide_row * 4 + k == wide_lane, 1.0, 0.0)
        rows = jnp.concatenate([v_ref[comp, :, k, :] for comp in range(3)], axis=0)
        part = dot_exact(rows, spread)
        acc = part if acc is None else acc + part

    def col(c):
        return slice(128 * c, 128 * (c + 1))

    for c in range(4):
        wind[c] = acc[:, col(c)]
        massx[c, 0:16, :] = mass_wide[:, col(c)]
        massx[c, 16:24, :] = rel_wide[:, col(c)]

    def side(ref, base, first, c):
        return ref[c, pl.ds(base + first, 4, stride=4), :]

    for message, first, c in ((msg_to_next, 3, 3), (msg_to_prev, 0, 0)):
        message[0:4, :] = side(wind, 0, first, c)
        message[4:8, :] = side(wind, 16, first, c)
        message[8:12, :] = side(massx, 0, first, c)
        message[12:16, :] = side(massx, 0, first, c)
        message[16:24, :] = massx[c, 16:24, :]

    pl.semaphore_wait(barrier, 4)
    send_a = remote(msg_to_next, msg_prev, msg_sem.at[0], {"elem": nxt})
    send_b = remote(msg_to_prev, msg_next, msg_sem.at[1], {"elem": prv})
    send_a.start()
    send_b.start()

    eye = jnp.where(iota((128, 128), 0) == iota((128, 128), 1), 1.0, 0.0).astype(bf16)
    for block in range(8):
        turned = dot_t(eye, t_ref[:, 128 * block : 128 * (block + 1)])
        tt[2 * block : 2 * block + 2, :, :] = turned.astype(bf16).reshape(2, 64, 512)

    pick = jnp.where(iota((512, 128), 0) == iota((512, 128), 1) * 4 + 3, 1.0, 0.0).astype(bf16)

    def x3_copy(q):
        return remote(x3_send.at[q], x3_recv.at[q], x3_sem.at[q], {"lev": below})

    def send_x3(q, carry):
        chunk = tt[:, pl.ds(pl.multiple_of(q * TQ, TQ), TQ), :].reshape(16 * TQ, 512)
        x3_send[q] = dot(chunk, pick).astype(bf16)
        x3_copy(q).start()
        return carry

    lax.fori_loop(0, CH, send_x3, 0)

    send_a.wait()
    send_b.wait()

    def pair(ref, first, c, rows):
        return jnp.concatenate([side(ref, base, first, c) for base in rows], axis=0)

    def after(a, b):
        return jnp.where(lane < 124, pltpu.roll(a, 124, 1), pltpu.roll(b, 124, 1))

    def before(a, b):
        return jnp.where(lane < 4, pltpu.roll(a, 4, 1), pltpu.roll(b, 4, 1))

    wind_east = [msg_prev[0:8, :]] + [pair(wind, 3, c, (0, 16)) for c in range(4)]
    wind_west = [pair(wind, 0, c, (0, 16)) for c in range(4)] + [msg_next[0:8, :]]
    mass_east = [msg_prev[8:16, :]] + [pair(massx, 3, c, (0, 0)) for c in range(4)]
    mass_west = [pair(massx, 0, c, (0, 0)) for c in range(4)] + [msg_next[8:16, :]]
    west_now = [wind_west[0]] + wind_west[:4]
    mass_now = [mass_west[0]] + mass_west[:4]
    part_east, part_west, shared = [], [], []
    for i in range(5):
        mass_next = after(mass_now[i], mass_west[i])
        wind_next = after(west_now[i], wind_west[i])
        inverse = 1.0 / (mass_east[i] + mass_next)
        part_east.append(mass_east[i] * inverse)
        part_west.append(mass_next * inverse)
        shared.append((mass_east[i] * wind_east[i] + mass_next * wind_next) * inverse)
    for c in range(4):
        new_west = before(shared[c], shared[c + 1])
        for comp in range(2):
            wind[c, pl.ds(16 * comp + 3, 4, stride=4), :] = shared[c + 1][4 * comp : 4 * comp + 4]
            wind[c, pl.ds(16 * comp, 4, stride=4), :] = new_west[4 * comp : 4 * comp + 4]

    node = iota((16, 1), 0)

    def point(i):
        out = jnp.full((16, 1), gll[3], f32)
        for a in range(3):
            out = jnp.where(i == a, gll[a], out)
        return out

    along_point = point(jnp.bitwise_and(node, 3))
    across_point = point(jnp.right_shift(node, 2))
    for c in range(4):
        along = basis(along_point - courant * wind[c, 0:16, :])
        across = basis(across_point - courant * wind[c, 16:32, :])
        for m in range(16):
            product = across[m // 4] * along[m % 4]
            wtab[c, 16 * m : 16 * m + 16, :] = product.astype(bf16).astype(f32)

    for c in range(4):
        wind[c, 32:48, :] = 1.0 / (1.0 + jnp.exp(-wind[c, 32:48, :]))

    def code(row, shift):
        return (row.astype(jnp.int32) + shift) * 4 + level

    ask_next = one_hot(256, code(msg_next[16:17, :], 0))
    ask_prev = one_hot(256, code(msg_prev[16:17, :], -192))
    pick_here = [one_hot(512, code(massx[c, 16:17, :], -64)) for c in range(4)]
    step_down = jnp.where(
        (iota((128, 128), 0) + 1 == iota((128, 128), 1)) & (level != 0), 1.0, 0.0
    ).astype(bf16)
    has_above = jnp.where(lev > 0, 1.0, 0.0)
    enter = [
        (jnp.where((iota((128, 128), 0) * 4 - 128 * c) == iota((128, 128), 1), 1.0, 0.0) * has_above).astype(bf16)
        for c in range(4)
    ]

    def halo_copies(q):
        return (
            remote(pack_next.at[q], halo_prev.at[q], halo_sem.at[q, 0], {"elem": nxt}),
            remote(pack_prev.at[q], halo_next.at[q], halo_sem.at[q, 1], {"elem": prv}),
        )

    def lift(q, carry):
        rows = pl.ds(pl.multiple_of(q * TQ, TQ), TQ)
        x3_copy(q).wait()
        extra = x3_recv[q]
        for c in range(4):
            here = tt[:, rows, col(c)].reshape(16 * TQ, 128)
            upper = dot(here, step_down) + dot(extra, enter[c])
            descent = jnp.broadcast_to(wind[c, 32:48, :][:, None, :], (16, TQ, 128)).reshape(16 * TQ, 128)
            value = (1.0 - descent) * here.astype(f32) + descent * upper
            lifted[q, :, col(c)] = value.astype(bf16)
        pack_next[q] = dot(lifted[q, :, 256:512], ask_next).astype(bf16)
        pack_prev[q] = dot(lifted[q, :, 0:256], ask_prev).astype(bf16)
        for copy in halo_copies(q):
            copy.start()
        return carry

    lax.fori_loop(0, CH, lift, 0)

    def gather(q, carry):
        for c in range(4):
            gath[q, c] = dot(lifted[q], pick_here[c]).astype(bf16)
        return carry

    lax.fori_loop(0, CH, gather, 0)

    def move(q, c, block):
        rows = pl.ds(pl.multiple_of(q * TQ, TQ), TQ)
        values = [block[TQ * m : TQ * (m + 1), :] for m in range(16)]
        for n in range(16):
            total_n = None
            for m in range(16):
                term = wtab[c, pl.ds(16 * m + n, 1), :] * values[m]
                total_n = term if total_n is None else total_n + term
            moved[c, n, rows, :] = total_n.astype(bf16)

    def inner(i, carry):
        q, c = i // 2, lax.rem(i, 2) + 1
        move(q, c, gath[q, c].astype(f32))
        return carry

    lax.fori_loop(0, 2 * CH, inner, 0)

    def outer(q, carry):
        for copy in halo_copies(q):
            copy.wait()
        move(q, 0, gath[q, 0].astype(f32) + halo_prev[q].astype(f32))
        move(q, 3, gath[q, 3].astype(f32) + halo_next[q].astype(f32))
        return carry

    lax.fori_loop(0, CH, outer, 0)

    east_end = jnp.concatenate([moved[3, 4 * j + 3] for j in range(4)], axis=0)
    west_end = jnp.concatenate([moved[0, 4 * j] for j in range(4)], axis=0)
    edge_to_next[...] = dot_t(eye[112:128], east_end).astype(bf16)
    edge_to_prev[...] = dot_t(eye[0:16], west_end).astype(bf16)
    edges[16:112, :] = jnp.zeros((96, 256), bf16)
    last_a = remote(edge_to_next, edges.at[112:128], edge_sem.at[0], {"elem": nxt})
    last_b = remote(edge_to_prev, edges.at[0:16], edge_sem.at[1], {"elem": prv})
    last_a.start()
    last_b.start()
    last_a.wait()
    last_b.wait()
    outside = jnp.transpose(edges[...].astype(f32))

    for j in range(4):
        mine = outside[64 * j : 64 * j + 64]
        east = [mine] + [moved[c, 4 * j + 3].astype(f32) for c in range(4)]
        west = [moved[c, 4 * j].astype(f32) for c in range(4)] + [mine]
        now = [west[0]] + west[:4]
        joint = []
        for i in range(5):
            joint.append(
                part_east[i][j : j + 1] * east[i] + part_west[i][j : j + 1] * after(now[i], west[i])
            )
        for c in range(4):
            moved[c, 4 * j + 3] = joint[c + 1].astype(bf16)
            moved[c, 4 * j] = before(joint[c], joint[c + 1]).astype(bf16)

    for c in range(4):
        o_ref[col(c), :] = dot_t(eye, moved[c].reshape(1024, 128)).astype(bf16)


def solution(mesh):
    peers_elem, peers_lev = mesh.shape["elem"], mesh.shape["lev"]

    def on_device(tracers, velocity, node_mass, source):
        elements, levels, columns = tracers.shape
        vmem = pl.BlockSpec(memory_space=pltpu.VMEM)
        out = pl.pallas_call(
            functools.partial(kernel, peers_elem, peers_lev, elements * peers_elem),
            out_shape=jax.ShapeDtypeStruct((elements * levels, columns), bf16),
            in_specs=[vmem] * 4,
            out_specs=vmem,
            scratch_shapes=[
                pltpu.VMEM((16, 64, 512), bf16),
                pltpu.VMEM((4, 48, 128), f32),
                pltpu.VMEM((4, 24, 128), f32),
                pltpu.VMEM((24, 128), f32),
                pltpu.VMEM((24, 128), f32),
                pltpu.VMEM((24, 128), f32),
                pltpu.VMEM((24, 128), f32),
                pltpu.VMEM((CH, 16 * TQ, 128), bf16),
                pltpu.VMEM((CH, 16 * TQ, 128), bf16),
                pltpu.VMEM((CH, 16 * TQ, 512), bf16),
                pltpu.VMEM((CH, 16 * TQ, 128), bf16),
                pltpu.VMEM((CH, 16 * TQ, 128), bf16),
                pltpu.VMEM((CH, 16 * TQ, 128), bf16),
                pltpu.VMEM((CH, 16 * TQ, 128), bf16),
                pltpu.VMEM((CH, 4, 16 * TQ, 128), bf16),
                pltpu.VMEM((4, 256, 128), f32),
                pltpu.VMEM((4, 16, 64, 128), bf16),
                pltpu.VMEM((16, 256), bf16),
                pltpu.VMEM((16, 256), bf16),
                pltpu.VMEM((128, 256), bf16),
                pltpu.SemaphoreType.DMA((2, 2)),
                pltpu.SemaphoreType.DMA((CH, 2)),
                pltpu.SemaphoreType.DMA((CH, 2, 2)),
                pltpu.SemaphoreType.DMA((2, 2)),
            ],
            compiler_params=pltpu.CompilerParams(collective_id=0, has_side_effects=True),
            name="transport",
        )(
            tracers.reshape(elements * levels, columns),
            velocity,
            node_mass,
            source.reshape(1, elements),
        )
        return out.reshape(elements, levels, columns)

    placed = (P("elem", "lev", None), P(None, None, "lev", "elem"), P(None, "elem"), P("elem"))
    return jax.shard_map(
        on_device, mesh=mesh, in_specs=placed, out_specs=P("elem", "lev", None), check_vma=False
    )
```

time: 110 us -> 45.5 us (0.41)
  starting transfers between devices: 43.9 us -> 0 us
  Pallas kernels: 0 us -> 40.9 us
  local copies, waits for them, and re-layouts: 33.3 us -> 4.37 us
  waiting for transfers between devices: 17.2 us -> 0 us
  other arithmetic: 10.9 us -> 0 us
  matrix products: 4.13 us -> 0 us
    ppermute x7 -> x0, starting transfers between devices: 43.9 us -> none  [the longest x4 32.7 us: from_behind(): lax.ppermute(array, axis, [(i, (i + by) % peers) for i in range(peers)])]
    pallas_call x0 -> x1, Pallas kernels: none -> 40.9 us  [on_device(): pl.pallas_call(functools.partial(kernel, peers_elem, peers_lev, elements...]
    ppermute x7 -> x0, waiting for transfers between devices: 17.2 us -> none  [the longest x1 10.1 us: with_halo(): lax.ppermute(tail, axis, [(i, (i + 1) % count) for i in range(count)])]
    gather x10 -> x0, local copies, waits for them, and re-layouts: 9.24 us -> none  [the longest x2 4.74 us: on_device(): blocks = jnp.take(padded, (relative + span) % total, axis=0)]
    convert_element_type x3 -> x0, local copies, waits for them, and re-layouts: 8.03 us -> none  [the longest x1 3.32 us: on_device(): moved = jnp.einsum('mnke,ekmt->eknt', table, blocks.reshape(shape_four),...]
    slice x26 -> x0, local copies, waits for them, and re-layouts: 5.71 us -> none  [the longest x1 2.64 us: on_device(): top_row = passed_along(tracers[:, levels_here - 1:, :], 'lev', 1)]
    dot_general x1 -> x0, matrix products: 4.13 us -> none  [on_device(): jnp.einsum('mnke,ekmt->eknt', table, blocks.reshape(shape_four), preferre...]
    convert_element_type x5 -> x0, other arithmetic: 3.83 us -> none  [the longest x1 3.49 us: on_device(): lifted = ((1.0 - descent_wide) * tracers.astype(jnp.float32) + descent_wi...]
  transfers between devices with their start and end apart: 7 -> 0, of which waited for: 4 -> 0; matrix products, arithmetic and copies ran while one was open for 18% -> 0% of each run, Pallas kernels for 0% -> 0%
where the time goes in v1:
time: 45.5 us; the launch traced here: 45.3 us
  Pallas kernels  40.9 us (90%)
  local copies, waits for them, and re-layouts  4.37 us (10%)
    pallas_call x1, Pallas kernels, on_device(): pl.pallas_call(functools.partial(kernel, peers_elem, peers_lev, elements...  40.9 us
    reshape x1, local copies, waits for them, and re-layouts, on_device(): return out.reshape(elements, levels, columns)  2.24 us
    reshape x1, local copies, waits for them, and re-layouts, on_device(): tracers.reshape(elements * levels, columns)  2.13 us

profile of v1, /device:TPU:2, one launch (start us, length us, event | category | flops | bytes accessed | tf_op | source)
XLA Modules:
  0.0 45.3 jit_solution(3678583805774862622)
XLA Ops:
  0.0 2.1 %reshape.9.t_ref = bf16[512,1024]{1,0:T(8,128)(2,1)} reshape(bf16[128,4,1024]{2,1,0:T(4,128)(2,1)} %param.4) | data formatting | bytes 2097152 | tf_op jit(solution)/shard_map/reshape | solution.py:336
  2.1 40.9 %transport.1 = bf16[512,1024]{1,0:T(8,128)(2,1)} custom-call(bf16[512,1024]{1,0:T(8,128)(2,1)} %reshape.9.t_ref, f32[3,16,4,128]{3,2,1,0:T(4,128)} %v_ref.1, f32[16,128]{1,0:T(8,128)} %mass_ref.1, s32[1,128]{1,0:T(1,128)} %bitcast.1), custom_call_target="tpu_custom_call" | custom-call | tf_op jit(solution)/shard_map/transport/pallas_call | solution.py:302
  43.1 2.2 %reshape.11 = bf16[128,4,1024]{2,1,0:T(4,128)(2,1)} reshape(bf16[512,1024]{1,0:T(8,128)(2,1)} %transport.1) | data formatting | bytes 2097152 | tf_op jit(solution)/shard_map/reshape | solution.py:341

commit v2 on v1

v2 whole, which is shorter than its diff:
```python
import functools

import jax
import jax.numpy as jnp
from jax import lax
from jax.experimental import pallas as pl
from jax.experimental.pallas import tpu as pltpu
from jax.sharding import PartitionSpec as P

MESH = pl.DeviceIdType.MESH
gll = (-1.0, -0.4472135954999579, 0.4472135954999579, 1.0)
courant = 0.15
f32 = jnp.float32
bf16 = jnp.bfloat16
CH = 4
TQ = 64 // CH


def dot(a, b):
    return lax.dot_general(a, b, (((1,), (0,)), ((), ())), preferred_element_type=f32)


def dot_t(a, b):
    return lax.dot_general(a, b, (((1,), (1,)), ((), ())), preferred_element_type=f32)


def three(x):
    top = x.astype(bf16)
    rest = x - top.astype(f32)
    middle = rest.astype(bf16)
    low = (rest - middle.astype(f32)).astype(bf16)
    return [top, middle, low]


def iota(shape, dim):
    return lax.broadcasted_iota(jnp.int32, shape, dim)


def one_hot(rows, code):
    return jnp.where(iota((rows, code.shape[1]), 0) == code, 1.0, 0.0).astype(bf16)


def basis(x):
    out = []
    for a in range(4):
        others = [b for b in range(4) if b != a]
        scale = 1.0
        for b in others:
            scale = scale / (gll[a] - gll[b])
        f = (x - gll[others[0]]) * (x - gll[others[1]]) * (x - gll[others[2]]) * scale
        out.append(f)
    return out


def kernel(
    peers_elem, peers_lev, total,
    t_hbm, v_hbm, mass_hbm, src_hbm, o_hbm,
    t_ref, v_ref, mass_ref, src_ref, out,
    tt, wind, massx, msg_to_next, msg_to_prev, msg_prev, msg_next,
    x3_send, x3_recv, lifted, pack_next, pack_prev, halo_prev, halo_next,
    gath, wtab, moved, edge_to_next, edge_to_prev, edges,
    enter, ask, pick_here, parts, late_west, late_east,
    in_sem, out_sem, msg_sem, x3_sem, halo_sem, edge_sem,
):
    elem = lax.axis_index("elem")
    lev = lax.axis_index("lev")
    nxt = lax.rem(elem + 1, peers_elem)
    prv = lax.rem(elem + peers_elem - 1, peers_elem)
    below = lax.rem(lev + 1, peers_lev)
    above = lax.rem(lev + peers_lev - 1, peers_lev)

    barrier = pltpu.get_barrier_semaphore()
    for target in ({"elem": nxt}, {"elem": prv}, {"lev": below}, {"lev": above}):
        pl.semaphore_signal(barrier, inc=1, device_id=target, device_id_type=MESH)

    def arrive(i, src, dst):
        copy = pltpu.make_async_copy(src, dst, in_sem.at[i])
        copy.start()
        return copy

    small = [arrive(1, v_hbm, v_ref), arrive(2, mass_hbm, mass_ref), arrive(3, src_hbm, src_ref)]
    large = arrive(0, t_hbm, t_ref)

    def remote(src, dst, sems, target):
        return pltpu.make_async_remote_copy(
            src_ref=src, dst_ref=dst, send_sem=sems.at[0], recv_sem=sems.at[1],
            device_id=target, device_id_type=MESH,
        )

    lane = iota((1, 128), 1)
    level = jnp.bitwise_and(lane, 3)

    def col(c):
        return slice(128 * c, 128 * (c + 1))

    for copy in small:
        copy.wait()
    rel = src_ref[...] - elem * 128 + 64
    rel = jnp.where(rel < 0, rel + total, rel)
    rel = jnp.where(rel >= total, rel - total, rel)
    rel16 = jnp.broadcast_to(rel.astype(f32), (16, 128)).astype(bf16)
    wide_lane = iota((128, 512), 1)
    wide_row = iota((128, 512), 0)
    spread_all = jnp.where(wide_row == jnp.right_shift(wide_lane, 2), 1.0, 0.0).astype(bf16)
    slow = dot(jnp.concatenate(three(mass_ref[...]) + [rel16], axis=0), spread_all)
    mass_wide = slow[0:16] + slow[16:32] + slow[32:48]
    rel_wide = slow[48:56]
    rows = jnp.concatenate(
        [
            jnp.concatenate([v_ref[comp, :, k, :] for comp in range(3)], axis=0)
            for k in range(4)
        ],
        axis=1,
    )
    spread = jnp.concatenate(
        [jnp.where(wide_row * 4 + k == wide_lane, 1.0, 0.0).astype(bf16) for k in range(4)], axis=0
    )
    fast = dot(jnp.concatenate(three(rows), axis=0), spread)
    fast = fast[0:48] + fast[48:96] + fast[96:144]
    for c in range(4):
        wind[c] = fast[:, col(c)]
        massx[c, 0:16, :] = mass_wide[:, col(c)]
        massx[c, 16:24, :] = rel_wide[:, col(c)]

    def side(ref, base, first, c):
        return ref[c, pl.ds(base + first, 4, stride=4), :]

    for message, first, c in ((msg_to_next, 3, 3), (msg_to_prev, 0, 0)):
        message[0:4, :] = side(wind, 0, first, c)
        message[4:8, :] = side(wind, 16, first, c)
        message[8:12, :] = side(massx, 0, first, c)
        message[12:16, :] = side(massx, 0, first, c)
        message[16:24, :] = massx[c, 16:24, :]

    large.wait()
    for block in range(8):
        turned = t_ref[:, :, 128 * block : 128 * (block + 1)].reshape(512, 128).T
        tt[2 * block : 2 * block + 2, :, :] = turned.reshape(2, 64, 512)

    pick = jnp.where(iota((512, 128), 0) == iota((512, 128), 1) * 4 + 3, 1.0, 0.0).astype(bf16)

    def x3_copy(q):
        return remote(x3_send.at[q], x3_recv.at[q], x3_sem.at[q], {"lev": below})

    def make_x3(q):
        chunk = tt[:, TQ * q : TQ * (q + 1), :].reshape(16 * TQ, 512)
        x3_send[q] = dot(chunk, pick).astype(bf16)

    for q in range(CH):
        make_x3(q)

    pl.semaphore_wait(barrier, 4)
    send_a = remote(msg_to_next, msg_prev, msg_sem.at[0], {"elem": nxt})
    send_b = remote(msg_to_prev, msg_next, msg_sem.at[1], {"elem": prv})
    send_a.start()
    send_b.start()
    for q in range(CH):
        x3_copy(q).start()

    for c in range(4):
        wind[c, 32:48, :] = 1.0 / (1.0 + jnp.exp(-wind[c, 32:48, :]))

    def code(row, shift):
        return (row.astype(jnp.int32) + shift) * 4 + level

    has_above = jnp.where(lev > 0, 1.0, 0.0)
    step_down = (iota((128, 128), 0) + 1 == iota((128, 128), 1)) & (level != 0)
    for c in range(4):
        enter[c, 0:128, :] = jnp.where(step_down, 1.0, 0.0).astype(bf16)
        entry = iota((128, 128), 0) * 4 - 128 * c == iota((128, 128), 1)
        enter[c, 128:256, :] = (jnp.where(entry, 1.0, 0.0) * has_above).astype(bf16)
    for i, pair in enumerate(((1, 2), (0, 3))):
        for side_of, c in enumerate(pair):
            pick_here[i, :, col(side_of)] = one_hot(512, code(massx[c, 16:17, :], -64))

    send_a.wait()
    send_b.wait()
    ask[0] = one_hot(256, code(msg_next[16:17, :], 0))
    ask[1] = one_hot(256, code(msg_prev[16:17, :], -192))

    def halo_copies(q):
        return (
            remote(pack_next.at[q], halo_prev.at[q], halo_sem.at[q, 0], {"elem": nxt}),
            remote(pack_prev.at[q], halo_next.at[q], halo_sem.at[q, 1], {"elem": prv}),
        )

    def lift(q, carry):
        rows = pl.ds(pl.multiple_of(q * TQ, TQ), TQ)
        x3_copy(q).wait()
        extra = x3_recv[q]
        for c in range(4):
            here = tt[:, rows, col(c)].reshape(16 * TQ, 128)
            upper = dot(jnp.concatenate([here, extra], axis=1), enter[c])
            descent = jnp.broadcast_to(wind[c, 32:48, :][:, None, :], (16, TQ, 128)).reshape(16 * TQ, 128)
            value = (1.0 - descent) * here.astype(f32) + descent * upper
            lifted[q, :, col(c)] = value.astype(bf16)
        pack_next[q] = dot(lifted[q, :, 256:512], ask[0]).astype(bf16)
        pack_prev[q] = dot(lifted[q, :, 0:256], ask[1]).astype(bf16)
        for copy in halo_copies(q):
            copy.start()
        return carry

    lax.fori_loop(0, CH, lift, 0)

    def pair(ref, first, c, rows):
        return jnp.concatenate([side(ref, base, first, c) for base in rows], axis=0)

    def after(a, b):
        return jnp.where(lane < 124, pltpu.roll(a, 124, 1), pltpu.roll(b, 124, 1))

    def before(a, b):
        return jnp.where(lane < 4, pltpu.roll(a, 4, 1), pltpu.roll(b, 4, 1))

    wind_east = [msg_prev[0:8, :]] + [pair(wind, 3, c, (0, 16)) for c in range(4)]
    wind_west = [pair(wind, 0, c, (0, 16)) for c in range(4)] + [msg_next[0:8, :]]
    mass_east = [msg_prev[8:16, :]] + [pair(massx, 3, c, (0, 0)) for c in range(4)]
    mass_west = [pair(massx, 0, c, (0, 0)) for c in range(4)] + [msg_next[8:16, :]]
    west_now = [wind_west[0]] + wind_west[:4]
    mass_now = [mass_west[0]] + mass_west[:4]
    shared = []
    for i in range(5):
        mass_next = after(mass_now[i], mass_west[i])
        wind_next = after(west_now[i], wind_west[i])
        inverse = 1.0 / (mass_east[i] + mass_next)
        parts[0, i] = mass_east[i] * inverse
        parts[1, i] = mass_next * inverse
        shared.append((mass_east[i] * wind_east[i] + mass_next * wind_next) * inverse)
    for c in range(4):
        new_west = before(shared[c], shared[c + 1])
        for comp in range(2):
            wind[c, pl.ds(16 * comp + 3, 4, stride=4), :] = shared[c + 1][4 * comp : 4 * comp + 4]
            wind[c, pl.ds(16 * comp, 4, stride=4), :] = new_west[4 * comp : 4 * comp + 4]

    node = iota((16, 1), 0)

    def point(i):
        value = jnp.full((16, 1), gll[3], f32)
        for a in range(3):
            value = jnp.where(i == a, gll[a], value)
        return value

    along_point = point(jnp.bitwise_and(node, 3))
    across_point = point(jnp.right_shift(node, 2))
    for c in range(4):
        along = basis(along_point - courant * wind[c, 0:16, :])
        across = basis(across_point - courant * wind[c, 16:32, :])
        for m in range(16):
            product = across[m // 4] * along[m % 4]
            wtab[c, 16 * m : 16 * m + 16, :] = product.astype(bf16).astype(f32)

    def gather(q, carry):
        for i, columns in enumerate(((1, 2), (0, 3))):
            block = dot(lifted[q], pick_here[i]).astype(bf16)
            for half, c in enumerate(columns):
                gath[q, c] = block[:, col(half)]
        return carry

    lax.fori_loop(0, CH, gather, 0)

    def move(q, c, block):
        rows = pl.ds(pl.multiple_of(q * TQ, TQ), TQ)
        values = [block[TQ * m : TQ * (m + 1), :] for m in range(16)]
        for n in range(16):
            total_n = None
            for m in range(16):
                term = wtab[c, pl.ds(16 * m + n, 1), :] * values[m]
                total_n = term if total_n is None else total_n + term
            moved[c, n, rows, :] = total_n.astype(bf16)

    def inner(i, carry):
        q, c = i // 2, lax.rem(i, 2) + 1
        move(q, c, gath[q, c].astype(f32))
        return carry

    lax.fori_loop(0, 2 * CH, inner, 0)

    def outer(q, carry):
        for copy in halo_copies(q):
            copy.wait()
        move(q, 0, gath[q, 0].astype(f32) + halo_prev[q].astype(f32))
        move(q, 3, gath[q, 3].astype(f32) + halo_next[q].astype(f32))
        return carry

    lax.fori_loop(0, CH, outer, 0)

    eye = jnp.where(iota((128, 128), 0) == iota((128, 128), 1), 1.0, 0.0).astype(bf16)
    east_end = jnp.concatenate([moved[3, 4 * j + 3] for j in range(4)], axis=0)
    west_end = jnp.concatenate([moved[0, 4 * j] for j in range(4)], axis=0)
    edge_to_next[...] = dot_t(eye[112:128], east_end).astype(bf16)
    edge_to_prev[...] = dot_t(eye[0:16], west_end).astype(bf16)
    last_a = remote(edge_to_next, edges.at[112:128], edge_sem.at[0], {"elem": nxt})
    last_b = remote(edge_to_prev, edges.at[0:16], edge_sem.at[1], {"elem": prv})
    last_a.start()
    last_b.start()
    edges[16:112, :] = jnp.zeros((96, 256), bf16)

    for j in range(4):
        east = [moved[c, 4 * j + 3].astype(f32) for c in range(4)]
        west = [moved[c, 4 * j].astype(f32) for c in range(4)]
        joint = []
        for c in range(3):
            joint.append(
                parts[0, c + 1, j : j + 1] * east[c]
                + parts[1, c + 1, j : j + 1] * after(west[c], west[c + 1])
            )
        tail = jnp.where(lane < 124, pltpu.roll(west[3], 124, 1), 0.0)
        late_east[j] = parts[0, 4, j : j + 1] * east[3] + parts[1, 4, j : j + 1] * tail
        front = parts[1, 0, j : j + 1] * pltpu.roll(west[0], 124, 1)
        late_west[j] = before(front, joint[0])
        for c in range(3):
            moved[c, 4 * j + 3] = joint[c].astype(bf16)
            follower = joint[c + 1] if c < 2 else late_east[j]
            moved[c + 1, 4 * j] = before(joint[c], follower).astype(bf16)

    leave = []

    def put(c):
        block = moved[c].reshape(1024, 128).T
        out[32 * c : 32 * c + 32] = block.reshape(32, 4, 1024)
        copy = pltpu.make_async_copy(
            out.at[32 * c : 32 * c + 32], o_hbm.at[32 * c : 32 * c + 32], out_sem.at[c]
        )
        copy.start()
        leave.append(copy)

    put(1)
    put(2)
    last_a.wait()
    last_b.wait()
    outside = jnp.transpose(edges[...].astype(f32))
    for j in range(4):
        mine = outside[64 * j : 64 * j + 64]
        reach = jnp.where(lane < 124, 0.0, pltpu.roll(mine, 124, 1))
        moved[3, 4 * j + 3] = (late_east[j] + parts[1, 4, j : j + 1] * reach).astype(bf16)
        reach = jnp.where(lane < 4, pltpu.roll(parts[0, 0, j : j + 1] * mine, 4, 1), 0.0)
        moved[0, 4 * j] = (late_west[j] + reach).astype(bf16)
    put(0)
    put(3)
    for copy in leave:
        copy.wait()


def solution(mesh):
    peers_elem, peers_lev = mesh.shape["elem"], mesh.shape["lev"]

    def on_device(tracers, velocity, node_mass, source):
        elements = tracers.shape[0]
        anywhere = pl.BlockSpec(memory_space=pl.ANY)
        out = pl.pallas_call(
            functools.partial(kernel, peers_elem, peers_lev, elements * peers_elem),
            out_shape=jax.ShapeDtypeStruct(tracers.shape, bf16),
            in_specs=[anywhere] * 4,
            out_specs=anywhere,
            scratch_shapes=[
                pltpu.VMEM(tracers.shape, bf16),
                pltpu.VMEM(velocity.shape, f32),
                pltpu.VMEM(node_mass.shape, f32),
                pltpu.VMEM((1, elements), jnp.int32),
                pltpu.VMEM(tracers.shape, bf16),
                pltpu.VMEM((16, 64, 512), bf16),
                pltpu.VMEM((4, 48, 128), f32),
                pltpu.VMEM((4, 24, 128), f32),
                pltpu.VMEM((24, 128), f32),
                pltpu.VMEM((24, 128), f32),
                pltpu.VMEM((24, 128), f32),
                pltpu.VMEM((24, 128), f32),
                pltpu.VMEM((CH, 16 * TQ, 128), bf16),
                pltpu.VMEM((CH, 16 * TQ, 128), bf16),
                pltpu.VMEM((CH, 16 * TQ, 512), bf16),
                pltpu.VMEM((CH, 16 * TQ, 128), bf16),
                pltpu.VMEM((CH, 16 * TQ, 128), bf16),
                pltpu.VMEM((CH, 16 * TQ, 128), bf16),
                pltpu.VMEM((CH, 16 * TQ, 128), bf16),
                pltpu.VMEM((CH, 4, 16 * TQ, 128), bf16),
                pltpu.VMEM((4, 256, 128), f32),
                pltpu.VMEM((4, 16, 64, 128), bf16),
                pltpu.VMEM((16, 256), bf16),
                pltpu.VMEM((16, 256), bf16),
                pltpu.VMEM((128, 256), bf16),
                pltpu.VMEM((4, 256, 128), bf16),
                pltpu.VMEM((2, 256, 128), bf16),
                pltpu.VMEM((2, 512, 256), bf16),
                pltpu.VMEM((2, 5, 8, 128), f32),
                pltpu.VMEM((4, 64, 128), f32),
                pltpu.VMEM((4, 64, 128), f32),
                pltpu.SemaphoreType.DMA((4,)),
                pltpu.SemaphoreType.DMA((4,)),
                pltpu.SemaphoreType.DMA((2, 2)),
                pltpu.SemaphoreType.DMA((CH, 2)),
                pltpu.SemaphoreType.DMA((CH, 2, 2)),
                pltpu.SemaphoreType.DMA((2, 2)),
            ],
            compiler_params=pltpu.CompilerParams(collective_id=0, has_side_effects=True),
            name="transport",
        )(
            tracers,
            velocity,
            node_mass,
            source.reshape(1, elements),
        )
        return out

    placed = (P("elem", "lev", None), P(None, None, "lev", "elem"), P(None, "elem"), P("elem"))
    return jax.shard_map(
        on_device, mesh=mesh, in_specs=placed, out_specs=P("elem", "lev", None), check_vma=False
    )
```

time: 45.5 us -> 41.3 us (0.908)
  the two profiles are of different devices: /device:TPU:2 before, /device:TPU:6 now
where the time goes in v2:
time: 41.3 us; the launch traced here: 41.1 us
  Pallas kernels  38.5 us (93%)
  local copies, waits for them, and re-layouts  2.56 us (6%)
    pallas_call x1, Pallas kernels, on_device(): pl.pallas_call(functools.partial(kernel, peers_elem, peers_lev, elements...  38.5 us
    unnamed x1, local copies, waits for them, and re-layouts  2.56 us

profile of v2, /device:TPU:6, one launch (start us, length us, event | category | flops | bytes accessed | tf_op | source)
XLA Modules:
  0.0 41.1 jit_solution(8248589812940413473)
XLA Ops:
  0.0 38.5 %transport.1 = bf16[128,4,1024]{2,1,0:T(4,128)(2,1)} custom-call(bf16[128,4,1024]{2,1,0:T(4,128)(2,1)} %t_hbm.1, f32[3,16,4,128]{3,2,1,0:T(4,128)} %v_hbm.1, f32[16,128]{1,0:T(8,128)} %mass_hbm.1, s32[1,128]{1,0:T(1,128)} %bitcast.1), custom_call_target="tpu_custom_call" | custom-call | tf_op jit(solution)/shard_map/transport/pallas_call | solution.py:349
  38.5 2.6 %copy.6 = bf16[128,4,1024]{2,1,0:T(4,128)(2,1)} copy(bf16[128,4,1024]{2,1,0:T(4,128)(2,1)} %transport.1) | data formatting | bytes 2097152

commit v3 on v2

--- a/solution.py
+++ b/solution.py
@@ -54,13 +54,13 @@
 
 def kernel(
     peers_elem, peers_lev, total,
-    t_hbm, v_hbm, mass_hbm, src_hbm, o_hbm,
-    t_ref, v_ref, mass_ref, src_ref, out,
+    t_hbm, v_hbm, mass_hbm, src_hbm, moved, outside, parts,
+    t_ref, v_ref, mass_ref, src_ref,
     tt, wind, massx, msg_to_next, msg_to_prev, msg_prev, msg_next,
     x3_send, x3_recv, lifted, pack_next, pack_prev, halo_prev, halo_next,
-    gath, wtab, moved, edge_to_next, edge_to_prev, edges,
-    enter, ask, pick_here, parts, late_west, late_east,
-    in_sem, out_sem, msg_sem, x3_sem, halo_sem, edge_sem,
+    gath, wtab, far_send, far_recv, far_pick, far_wtab,
+    enter, ask, pick_here,
+    in_sem, msg_sem, x3_sem, halo_sem, far_sem,
 ):
     elem = lax.axis_index("elem")
     lev = lax.axis_index("lev")
@@ -142,12 +142,10 @@
     def x3_copy(q):
         return remote(x3_send.at[q], x3_recv.at[q], x3_sem.at[q], {"lev": below})
 
-    def make_x3(q):
-        chunk = tt[:, TQ * q : TQ * (q + 1), :].reshape(16 * TQ, 512)
-        x3_send[q] = dot(chunk, pick).astype(bf16)
-
+    chosen = dot(tt[...].reshape(1024, 512), pick).astype(bf16).reshape(16, 64, 128)
     for q in range(CH):
-        make_x3(q)
+        x3_send[q] = chosen[:, TQ * q : TQ * (q + 1), :].reshape(16 * TQ, 128)
+        far_recv[q, 16:112, :] = jnp.zeros((96, 16 * TQ), bf16)
 
     pl.semaphore_wait(barrier, 4)
     send_a = remote(msg_to_next, msg_prev, msg_sem.at[0], {"elem": nxt})
@@ -173,18 +171,20 @@
         for side_of, c in enumerate(pair):
             pick_here[i, :, col(side_of)] = one_hot(512, code(massx[c, 16:17, :], -64))
 
-    send_a.wait()
-    send_b.wait()
-    ask[0] = one_hot(256, code(msg_next[16:17, :], 0))
-    ask[1] = one_hot(256, code(msg_prev[16:17, :], -192))
-
-    def halo_copies(q):
+    eye = jnp.where(iota((128, 128), 0) == iota((128, 128), 1), 1.0, 0.0).astype(bf16)
+    far_pick[0:16, :] = dot_t(eye[0:16], pick_here[1, :, 0:128]).astype(bf16)
+    far_pick[16:32, :] = dot_t(eye[112:128], pick_here[1, :, 128:256]).astype(bf16)
+
+    def sends(q):
+        ahead, back = {"elem": nxt}, {"elem": prv}
         return (
-            remote(pack_next.at[q], halo_prev.at[q], halo_sem.at[q, 0], {"elem": nxt}),
-            remote(pack_prev.at[q], halo_next.at[q], halo_sem.at[q, 1], {"elem": prv}),
+            remote(far_send.at[q, 0], far_recv.at[q, 0:16], far_sem.at[q, 0], back),
+            remote(far_send.at[q, 1], far_recv.at[q, 112:128], far_sem.at[q, 1], ahead),
+            remote(pack_next.at[q], halo_prev.at[q], halo_sem.at[q, 0], ahead),
+            remote(pack_prev.at[q], halo_next.at[q], halo_sem.at[q, 1], back),
         )
 
-    def lift(q, carry):
+    def lift(q):
         rows = pl.ds(pl.multiple_of(q * TQ, TQ), TQ)
         x3_copy(q).wait()
         extra = x3_recv[q]
@@ -194,13 +194,29 @@
             descent = jnp.broadcast_to(wind[c, 32:48, :][:, None, :], (16, TQ, 128)).reshape(16 * TQ, 128)
             value = (1.0 - descent) * here.astype(f32) + descent * upper
             lifted[q, :, col(c)] = value.astype(bf16)
+
+    def pack(q):
         pack_next[q] = dot(lifted[q, :, 256:512], ask[0]).astype(bf16)
         pack_prev[q] = dot(lifted[q, :, 0:256], ask[1]).astype(bf16)
-        for copy in halo_copies(q):
+        far = dot_t(far_pick[...], lifted[q]).astype(bf16)
+        far_send[q, 0] = far[0:16]
+        far_send[q, 1] = far[16:32]
+        for copy in sends(q):
             copy.start()
+
+    lift(0)
+    send_a.wait()
+    send_b.wait()
+    ask[0] = one_hot(256, code(msg_next[16:17, :], 0))
+    ask[1] = one_hot(256, code(msg_prev[16:17, :], -192))
+
+    def step(q, carry):
+        pack(q)
+        lift(q + 1)
         return carry
 
-    lax.fori_loop(0, CH, lift, 0)
+    lax.fori_loop(0, CH - 1, step, 0)
+    pack(CH - 1)
 
     def pair(ref, first, c, rows):
         return jnp.concatenate([side(ref, base, first, c) for base in rows], axis=0)
@@ -234,7 +250,7 @@
     node = iota((16, 1), 0)
 
     def point(i):
-        value = jnp.full((16, 1), gll[3], f32)
+        value = jnp.full(i.shape, gll[3], f32)
         for a in range(3):
             value = jnp.where(i == a, gll[a], value)
         return value
@@ -247,6 +263,13 @@
         for m in range(16):
             product = across[m // 4] * along[m % 4]
             wtab[c, 16 * m : 16 * m + 16, :] = product.astype(bf16).astype(f32)
+
+    beyond = jnp.where(lane < 4, pltpu.roll(shared[4], 4, 1), shared[0])
+    along = basis(jnp.where(lane < 4, gll[0], gll[3]) - courant * beyond[0:4])
+    across = basis(point(iota((4, 1), 0)) - courant * beyond[4:8])
+    for m in range(16):
+        product = across[m // 4] * along[m % 4]
+        far_wtab[4 * m : 4 * m + 4, :] = product.astype(bf16).astype(f32)
 
     def gather(q, carry):
         for i, columns in enumerate(((1, 2), (0, 3))):
@@ -275,67 +298,56 @@
     lax.fori_loop(0, 2 * CH, inner, 0)
 
     def outer(q, carry):
-        for copy in halo_copies(q):
+        rows = pl.ds(pl.multiple_of(q * TQ, TQ), TQ)
+        for copy in sends(q):
             copy.wait()
         move(q, 0, gath[q, 0].astype(f32) + halo_prev[q].astype(f32))
         move(q, 3, gath[q, 3].astype(f32) + halo_next[q].astype(f32))
+        here = jnp.where(lane < 64, pack_next[q].astype(f32), pack_prev[q].astype(f32))
+        block = jnp.transpose(far_recv[q].astype(f32))
+        block = jnp.where((lane < 4) | (lane >= 124), block + here, 0.0)
+        values = [block[TQ * m : TQ * (m + 1), :] for m in range(16)]
+        for j in range(4):
+            total_j = None
+            for m in range(16):
+                term = far_wtab[pl.ds(4 * m + j, 1), :] * values[m]
+                total_j = term if total_j is None else total_j + term
+            outside[j, rows, :] = total_j.astype(bf16)
         return carry
 
     lax.fori_loop(0, CH, outer, 0)
 
-    eye = jnp.where(iota((128, 128), 0) == iota((128, 128), 1), 1.0, 0.0).astype(bf16)
-    east_end = jnp.concatenate([moved[3, 4 * j + 3] for j in range(4)], axis=0)
-    west_end = jnp.concatenate([moved[0, 4 * j] for j in range(4)], axis=0)
-    edge_to_next[...] = dot_t(eye[112:128], east_end).astype(bf16)
-    edge_to_prev[...] = dot_t(eye[0:16], west_end).astype(bf16)
-    last_a = remote(edge_to_next, edges.at[112:128], edge_sem.at[0], {"elem": nxt})
-    last_b = remote(edge_to_prev, edges.at[0:16], edge_sem.at[1], {"elem": prv})
-    last_a.start()
-    last_b.start()
-    edges[16:112, :] = jnp.zeros((96, 256), bf16)
-
+
+def share_kernel(moved, outside, parts, o_hbm, out, out_sem):
+    lane = iota((1, 128), 1)
+
+    def after(a, b):
+        return jnp.where(lane < 124, pltpu.roll(a, 124, 1), pltpu.roll(b, 124, 1))
+
+    def before(a, b):
+        return jnp.where(lane < 4, pltpu.roll(a, 4, 1), pltpu.roll(b, 4, 1))
+
+    leave = []
     for j in range(4):
-        east = [moved[c, 4 * j + 3].astype(f32) for c in range(4)]
-        west = [moved[c, 4 * j].astype(f32) for c in range(4)]
-        joint = []
-        for c in range(3):
-            joint.append(
-                parts[0, c + 1, j : j + 1] * east[c]
-                + parts[1, c + 1, j : j + 1] * after(west[c], west[c + 1])
-            )
-        tail = jnp.where(lane < 124, pltpu.roll(west[3], 124, 1), 0.0)
-        late_east[j] = parts[0, 4, j : j + 1] * east[3] + parts[1, 4, j : j + 1] * tail
-        front = parts[1, 0, j : j + 1] * pltpu.roll(west[0], 124, 1)
-        late_west[j] = before(front, joint[0])
-        for c in range(3):
-            moved[c, 4 * j + 3] = joint[c].astype(bf16)
-            follower = joint[c + 1] if c < 2 else late_east[j]
-            moved[c + 1, 4 * j] = before(joint[c], follower).astype(bf16)
-
-    leave = []
-
-    def put(c):
-        block = moved[c].reshape(1024, 128).T
-        out[32 * c : 32 * c + 32] = block.reshape(32, 4, 1024)
-        copy = pltpu.make_async_copy(
-            out.at[32 * c : 32 * c + 32], o_hbm.at[32 * c : 32 * c + 32], out_sem.at[c]
-        )
+        mine = outside[j].astype(f32)
+        east = [mine] + [moved[c, 4 * j + 3].astype(f32) for c in range(4)]
+        west = [moved[c, 4 * j].astype(f32) for c in range(4)] + [mine]
+        now = [west[0]] + west[:4]
+        joint = [
+            parts[0, i, j : j + 1] * east[i] + parts[1, i, j : j + 1] * after(now[i], west[i])
+            for i in range(5)
+        ]
+        for c in range(4):
+            first = before(joint[c], joint[c + 1]).astype(bf16)
+            last = joint[c + 1].astype(bf16)
+            for half, pair in enumerate(((first, moved[c, 4 * j + 1]), (moved[c, 4 * j + 2], last))):
+                turned = jnp.concatenate(pair, axis=0).T
+                place = slice(256 * j + 128 * half, 256 * j + 128 * half + 128)
+                out[32 * c : 32 * c + 32, :, place] = turned.reshape(32, 4, 128)
+        place = slice(256 * j, 256 * j + 256)
+        copy = pltpu.make_async_copy(out.at[:, :, place], o_hbm.at[:, :, place], out_sem.at[j])
         copy.start()
         leave.append(copy)
-
-    put(1)
-    put(2)
-    last_a.wait()
-    last_b.wait()
-    outside = jnp.transpose(edges[...].astype(f32))
-    for j in range(4):
-        mine = outside[64 * j : 64 * j + 64]
-        reach = jnp.where(lane < 124, 0.0, pltpu.roll(mine, 124, 1))
-        moved[3, 4 * j + 3] = (late_east[j] + parts[1, 4, j : j + 1] * reach).astype(bf16)
-        reach = jnp.where(lane < 4, pltpu.roll(parts[0, 0, j : j + 1] * mine, 4, 1), 0.0)
-        moved[0, 4 * j] = (late_west[j] + reach).astype(bf16)
-    put(0)
-    put(3)
     for copy in leave:
         copy.wait()
 
@@ -346,17 +358,21 @@
     def on_device(tracers, velocity, node_mass, source):
         elements = tracers.shape[0]
         anywhere = pl.BlockSpec(memory_space=pl.ANY)
-        out = pl.pallas_call(
+        vmem = pl.BlockSpec(memory_space=pltpu.VMEM)
+        pieces = pl.pallas_call(
             functools.partial(kernel, peers_elem, peers_lev, elements * peers_elem),
-            out_shape=jax.ShapeDtypeStruct(tracers.shape, bf16),
+            out_shape=(
+                pltpu.VMEM((4, 16, 64, 128), bf16),
+                pltpu.VMEM((4, 64, 128), bf16),
+                pltpu.VMEM((2, 5, 8, 128), f32),
+            ),
             in_specs=[anywhere] * 4,
-            out_specs=anywhere,
+            out_specs=(vmem, vmem, vmem),
             scratch_shapes=[
                 pltpu.VMEM(tracers.shape, bf16),
                 pltpu.VMEM(velocity.shape, f32),
                 pltpu.VMEM(node_mass.shape, f32),
                 pltpu.VMEM((1, elements), jnp.int32),
-                pltpu.VMEM(tracers.shape, bf16),
                 pltpu.VMEM((16, 64, 512), bf16),
                 pltpu.VMEM((4, 48, 128), f32),
                 pltpu.VMEM((4, 24, 128), f32),
@@ -373,32 +389,31 @@
                 pltpu.VMEM((CH, 16 * TQ, 128), bf16),
                 pltpu.VMEM((CH, 4, 16 * TQ, 128), bf16),
                 pltpu.VMEM((4, 256, 128), f32),
-                pltpu.VMEM((4, 16, 64, 128), bf16),
-                pltpu.VMEM((16, 256), bf16),
-                pltpu.VMEM((16, 256), bf16),
-                pltpu.VMEM((128, 256), bf16),
+                pltpu.VMEM((CH, 2, 16, 16 * TQ), bf16),
+                pltpu.VMEM((CH, 128, 16 * TQ), bf16),
+                pltpu.VMEM((32, 512), bf16),
+                pltpu.VMEM((64, 128), f32),
                 pltpu.VMEM((4, 256, 128), bf16),
                 pltpu.VMEM((2, 256, 128), bf16),
                 pltpu.VMEM((2, 512, 256), bf16),
-                pltpu.VMEM((2, 5, 8, 128), f32),
-                pltpu.VMEM((4, 64, 128), f32),
-                pltpu.VMEM((4, 64, 128), f32),
-                pltpu.SemaphoreType.DMA((4,)),
                 pltpu.SemaphoreType.DMA((4,)),
                 pltpu.SemaphoreType.DMA((2, 2)),
                 pltpu.SemaphoreType.DMA((CH, 2)),
                 pltpu.SemaphoreType.DMA((CH, 2, 2)),
-                pltpu.SemaphoreType.DMA((2, 2)),
+                pltpu.SemaphoreType.DMA((CH, 2, 2)),
             ],
             compiler_params=pltpu.CompilerParams(collective_id=0, has_side_effects=True),
             name="transport",
-        )(
-            tracers,
-            velocity,
-            node_mass,
-            source.reshape(1, elements),
-        )
-        return out
+        )(tracers, velocity, node_mass, source.reshape(1, elements))
+        return pl.pallas_call(
+            share_kernel,
+            out_shape=jax.ShapeDtypeStruct(tracers.shape, bf16),
+            in_specs=[vmem] * 3,
+            out_specs=anywhere,
+            scratch_shapes=[pltpu.VMEM(tracers.shape, bf16), pltpu.SemaphoreType.DMA((4,))],
+            compiler_params=pltpu.CompilerParams(vmem_limit_bytes=24 * 2**20),
+            name="share",
+        )(*pieces)
 
     placed = (P("elem", "lev", None), P(None, None, "lev", "elem"), P(None, "elem"), P("elem"))
     return jax.shard_map(

time: 41.3 us -> 35.9 us (0.87)
  Pallas kernels: 38.5 us -> 35.8 us
  local copies, waits for them, and re-layouts: 2.56 us -> 0 us
    pallas_call x1, Pallas kernels: 38.5 us -> 34 us  [on_device(): pl.pallas_call(functools.partial(kernel, peers_elem, peers_lev, elements...]
    unnamed x1 -> x0, local copies, waits for them, and re-layouts: 2.56 us -> none
    pallas_call x0 -> x1, Pallas kernels: none -> 1.77 us  [on_device(): pl.pallas_call(share_kernel, out_shape=jax.ShapeDtypeStruct(tracers.shape...]
where the time goes in v3:
time: 35.9 us; the launch traced here: 35.8 us
  Pallas kernels  35.8 us (100%)
    pallas_call x1, Pallas kernels, on_device(): pl.pallas_call(functools.partial(kernel, peers_elem, peers_lev, elements...  34 us
    pallas_call x1, Pallas kernels, on_device(): pl.pallas_call(share_kernel, out_shape=jax.ShapeDtypeStruct(tracers.shape...  1.77 us

profile of v3, /device:TPU:6, one launch (start us, length us, event | category | flops | bytes accessed | tf_op | source)
XLA Modules:
  0.0 35.8 jit_solution(10290109572140845614)
XLA Ops:
  0.0 34.0 %transport.1 = (bf16[4,16,64,128]{3,2,1,0:T(8,128)(2,1)S(1)}, bf16[4,64,128]{2,1,0:T(8,128)(2,1)S(1)}, f32[2,5,8,128]{3,2,1,0:T(8,128)S(1)}) custom-call(bf16[128,4,1024]{2,1,0:T(4,128)(2,1)} %t_hbm.1, f32[3,16,4,128]{3,2,1,0:T(4,128)} %v_hbm.1, f32[16,128]{1,0:T(8,128)} %mass_hbm.1, s32[1,128]{1,0:T(1,128)} %bitcast.1), custom_call_target="tpu_custom_call" | custom-call | tf_op jit(solution)/shard_map/transport/pallas_call | solution.py:362
  34.0 1.8 %share.1 = bf16[128,4,1024]{2,1,0:T(4,128)(2,1)} custom-call(bf16[4,16,64,128]{3,2,1,0:T(8,128)(2,1)S(1)} %get-tuple-element.8.moved, bf16[4,64,128]{2,1,0:T(8,128)(2,1)S(1)} %get-tuple-element.9.outside, f32[2,5,8,128]{3,2,1,0:T(8,128)S(1)} %get-tuple-element.10.parts), custom_call_target="tpu_custom_call" | custom-call | tf_op jit(solution)/shard_map/share/pallas_call | solution.py:408

commit v4 on v3

--- a/solution.py
+++ b/solution.py
@@ -59,8 +59,8 @@
     tt, wind, massx, msg_to_next, msg_to_prev, msg_prev, msg_next,
     x3_send, x3_recv, lifted, pack_next, pack_prev, halo_prev, halo_next,
     gath, wtab, far_send, far_recv, far_pick, far_wtab,
-    enter, ask, pick_here,
-    in_sem, msg_sem, x3_sem, halo_sem, far_sem,
+    enter, ask, pick_here, full_prev, full_next,
+    in_sem, msg_sem, x3_sem, halo_sem, far_sem, full_sem,
 ):
     elem = lax.axis_index("elem")
     lev = lax.axis_index("lev")
@@ -175,14 +175,22 @@
     far_pick[0:16, :] = dot_t(eye[0:16], pick_here[1, :, 0:128]).astype(bf16)
     far_pick[16:32, :] = dot_t(eye[112:128], pick_here[1, :, 128:256]).astype(bf16)
 
-    def sends(q):
-        ahead, back = {"elem": nxt}, {"elem": prv}
+    ahead, back = {"elem": nxt}, {"elem": prv}
+
+    def from_next(q):
+        return remote(pack_prev.at[q], halo_next.at[q], halo_sem.at[q, 1], back)
+
+    def from_prev(q):
+        return remote(pack_next.at[q], halo_prev.at[q], halo_sem.at[q, 0], ahead)
+
+    def far_copies(q):
         return (
             remote(far_send.at[q, 0], far_recv.at[q, 0:16], far_sem.at[q, 0], back),
             remote(far_send.at[q, 1], far_recv.at[q, 112:128], far_sem.at[q, 1], ahead),
-            remote(pack_next.at[q], halo_prev.at[q], halo_sem.at[q, 0], ahead),
-            remote(pack_prev.at[q], halo_next.at[q], halo_sem.at[q, 1], back),
         )
+
+    full_ahead = remote(lifted.at[0, :, 256:512], full_prev, full_sem.at[0], ahead)
+    full_back = remote(lifted.at[0, :, 0:256], full_next, full_sem.at[1], back)
 
     def lift(q):
         rows = pl.ds(pl.multiple_of(q * TQ, TQ), TQ)
@@ -195,28 +203,43 @@
             value = (1.0 - descent) * here.astype(f32) + descent * upper
             lifted[q, :, col(c)] = value.astype(bf16)
 
+    def far_out(q):
+        far = dot_t(far_pick[...], lifted[q]).astype(bf16)
+        far_send[q, 0] = far[0:16]
+        far_send[q, 1] = far[16:32]
+        for copy in far_copies(q):
+            copy.start()
+
     def pack(q):
         pack_next[q] = dot(lifted[q, :, 256:512], ask[0]).astype(bf16)
         pack_prev[q] = dot(lifted[q, :, 0:256], ask[1]).astype(bf16)
-        far = dot_t(far_pick[...], lifted[q]).astype(bf16)
-        far_send[q, 0] = far[0:16]
-        far_send[q, 1] = far[16:32]
-        for copy in sends(q):
-            copy.start()
 
     lift(0)
+    full_ahead.start()
+    full_back.start()
+    far_out(0)
+
+    def lift_more(q, carry):
+        lift(q)
+        far_out(q)
+        return carry
+
+    lax.fori_loop(1, CH, lift_more, 0)
     send_a.wait()
     send_b.wait()
     ask[0] = one_hot(256, code(msg_next[16:17, :], 0))
     ask[1] = one_hot(256, code(msg_prev[16:17, :], -192))
 
-    def step(q, carry):
+    def answer(q, carry):
         pack(q)
-        lift(q + 1)
-        return carry
-
-    lax.fori_loop(0, CH - 1, step, 0)
-    pack(CH - 1)
+        from_prev(q).start()
+        from_next(q).start()
+        return carry
+
+    lax.fori_loop(1, CH, answer, 0)
+    pack(0)
+    ask[2] = one_hot(256, code(massx[0, 16:17, :], 0))
+    ask[3] = one_hot(256, code(massx[3, 16:17, :], -192))
 
     def pair(ref, first, c, rows):
         return jnp.concatenate([side(ref, base, first, c) for base in rows], axis=0)
@@ -297,12 +320,31 @@
 
     lax.fori_loop(0, 2 * CH, inner, 0)
 
-    def outer(q, carry):
+    full_back.wait()
+    halo_next[0] = dot(full_next[...], ask[3]).astype(bf16)
+
+    def outer_east(q, carry):
+        @pl.when(q > 0)
+        def _():
+            from_next(q).wait()
+
+        move(q, 3, gath[q, 3].astype(f32) + halo_next[q].astype(f32))
+        return carry
+
+    lax.fori_loop(0, CH, outer_east, 0)
+    full_ahead.wait()
+    halo_prev[0] = dot(full_prev[...], ask[2]).astype(bf16)
+
+    def outer_west(q, carry):
         rows = pl.ds(pl.multiple_of(q * TQ, TQ), TQ)
-        for copy in sends(q):
+        for copy in far_copies(q):
             copy.wait()
+
+        @pl.when(q > 0)
+        def _():
+            from_prev(q).wait()
+
         move(q, 0, gath[q, 0].astype(f32) + halo_prev[q].astype(f32))
-        move(q, 3, gath[q, 3].astype(f32) + halo_next[q].astype(f32))
         here = jnp.where(lane < 64, pack_next[q].astype(f32), pack_prev[q].astype(f32))
         block = jnp.transpose(far_recv[q].astype(f32))
         block = jnp.where((lane < 4) | (lane >= 124), block + here, 0.0)
@@ -315,7 +357,7 @@
             outside[j, rows, :] = total_j.astype(bf16)
         return carry
 
-    lax.fori_loop(0, CH, outer, 0)
+    lax.fori_loop(0, CH, outer_west, 0)
 
 
 def share_kernel(moved, outside, parts, o_hbm, out, out_sem):
@@ -394,13 +436,16 @@
                 pltpu.VMEM((32, 512), bf16),
                 pltpu.VMEM((64, 128), f32),
                 pltpu.VMEM((4, 256, 128), bf16),
-                pltpu.VMEM((2, 256, 128), bf16),
+                pltpu.VMEM((4, 256, 128), bf16),
                 pltpu.VMEM((2, 512, 256), bf16),
+                pltpu.VMEM((16 * TQ, 256), bf16),
+                pltpu.VMEM((16 * TQ, 256), bf16),
                 pltpu.SemaphoreType.DMA((4,)),
                 pltpu.SemaphoreType.DMA((2, 2)),
                 pltpu.SemaphoreType.DMA((CH, 2)),
                 pltpu.SemaphoreType.DMA((CH, 2, 2)),
                 pltpu.SemaphoreType.DMA((CH, 2, 2)),
+                pltpu.SemaphoreType.DMA((2, 2)),
             ],
             compiler_params=pltpu.CompilerParams(collective_id=0, has_side_effects=True),
             name="transport",

time: 35.9 us -> 34.9 us (0.972)
  Pallas kernels: 35.8 us -> 34.8 us
    pallas_call x1, Pallas kernels: 34 us -> 33 us  [on_device(): pl.pallas_call(functools.partial(kernel, peers_elem, peers_lev, elements...]
where the time goes in v4:
time: 34.9 us; the launch traced here: 34.8 us
  Pallas kernels  34.8 us (100%)
    pallas_call x1, Pallas kernels, on_device(): pl.pallas_call(functools.partial(kernel, peers_elem, peers_lev, elements...  33 us
    pallas_call x1, Pallas kernels, on_device(): pl.pallas_call(share_kernel, out_shape=jax.ShapeDtypeStruct(tracers.shape...  1.77 us

profile of v4, /device:TPU:6, one launch (start us, length us, event | category | flops | bytes accessed | tf_op | source)
XLA Modules:
  0.0 34.8 jit_solution(12552508134099685075)
XLA Ops:
  0.0 33.0 %transport.1 = (bf16[4,16,64,128]{3,2,1,0:T(8,128)(2,1)S(1)}, bf16[4,64,128]{2,1,0:T(8,128)(2,1)S(1)}, f32[2,5,8,128]{3,2,1,0:T(8,128)S(1)}) custom-call(bf16[128,4,1024]{2,1,0:T(4,128)(2,1)} %t_hbm.1, f32[3,16,4,128]{3,2,1,0:T(4,128)} %v_hbm.1, f32[16,128]{1,0:T(8,128)} %mass_hbm.1, s32[1,128]{1,0:T(1,128)} %bitcast.1), custom_call_target="tpu_custom_call" | custom-call | tf_op jit(solution)/shard_map/transport/pallas_call | solution.py:404
  33.0 1.8 %share.1 = bf16[128,4,1024]{2,1,0:T(4,128)(2,1)} custom-call(bf16[4,16,64,128]{3,2,1,0:T(8,128)(2,1)S(1)} %get-tuple-element.8.moved, bf16[4,64,128]{2,1,0:T(8,128)(2,1)S(1)} %get-tuple-element.9.outside, f32[2,5,8,128]{3,2,1,0:T(8,128)S(1)} %get-tuple-element.10.parts), custom_call_target="tpu_custom_call" | custom-call | tf_op jit(solution)/shard_map/share/pallas_call | solution.py:453

commit v5 on v4

--- a/solution.py
+++ b/solution.py
@@ -54,12 +54,12 @@
 
 def kernel(
     peers_elem, peers_lev, total,
-    t_hbm, v_hbm, mass_hbm, src_hbm, moved, outside, parts,
+    t_hbm, v_hbm, mass_hbm, src_hbm, first_col, west_raw, outside, parts, rest,
     t_ref, v_ref, mass_ref, src_ref,
     tt, wind, massx, msg_to_next, msg_to_prev, msg_prev, msg_next,
     x3_send, x3_recv, lifted, pack_next, pack_prev, halo_prev, halo_next,
     gath, wtab, far_send, far_recv, far_pick, far_wtab,
-    enter, ask, pick_here, full_prev, full_next,
+    enter, ask, pick_here, full_prev, full_next, moved,
     in_sem, msg_sem, x3_sem, halo_sem, far_sem, full_sem,
 ):
     elem = lax.axis_index("elem")
@@ -303,7 +303,7 @@
 
     lax.fori_loop(0, CH, gather, 0)
 
-    def move(q, c, block):
+    def move(q, c, block, place):
         rows = pl.ds(pl.multiple_of(q * TQ, TQ), TQ)
         values = [block[TQ * m : TQ * (m + 1), :] for m in range(16)]
         for n in range(16):
@@ -311,11 +311,11 @@
             for m in range(16):
                 term = wtab[c, pl.ds(16 * m + n, 1), :] * values[m]
                 total_n = term if total_n is None else total_n + term
-            moved[c, n, rows, :] = total_n.astype(bf16)
+            place[n, rows, :] = total_n.astype(bf16)
 
     def inner(i, carry):
         q, c = i // 2, lax.rem(i, 2) + 1
-        move(q, c, gath[q, c].astype(f32))
+        move(q, c, gath[q, c].astype(f32), moved.at[c])
         return carry
 
     lax.fori_loop(0, 2 * CH, inner, 0)
@@ -328,23 +328,14 @@
         def _():
             from_next(q).wait()
 
-        move(q, 3, gath[q, 3].astype(f32) + halo_next[q].astype(f32))
+        move(q, 3, gath[q, 3].astype(f32) + halo_next[q].astype(f32), moved.at[3])
         return carry
 
     lax.fori_loop(0, CH, outer_east, 0)
-    full_ahead.wait()
-    halo_prev[0] = dot(full_prev[...], ask[2]).astype(bf16)
-
-    def outer_west(q, carry):
+    def beyond_ends(q, carry):
         rows = pl.ds(pl.multiple_of(q * TQ, TQ), TQ)
         for copy in far_copies(q):
             copy.wait()
-
-        @pl.when(q > 0)
-        def _():
-            from_prev(q).wait()
-
-        move(q, 0, gath[q, 0].astype(f32) + halo_prev[q].astype(f32))
         here = jnp.where(lane < 64, pack_next[q].astype(f32), pack_prev[q].astype(f32))
         block = jnp.transpose(far_recv[q].astype(f32))
         block = jnp.where((lane < 4) | (lane >= 124), block + here, 0.0)
@@ -357,11 +348,48 @@
             outside[j, rows, :] = total_j.astype(bf16)
         return carry
 
+    lax.fori_loop(0, CH, beyond_ends, 0)
+
+    for j in range(4):
+        west_raw[j] = moved[1, 4 * j]
+        west = [moved[c, 4 * j].astype(f32) for c in (1, 2, 3)] + [outside[j].astype(f32)]
+        joint = []
+        for i, c in enumerate((1, 2, 3)):
+            joint.append(
+                parts[0, c + 1, j : j + 1] * moved[c, 4 * j + 3].astype(f32)
+                + parts[1, c + 1, j : j + 1] * after(west[i], west[i + 1])
+            )
+        for i, c in enumerate((1, 2, 3)):
+            first = (before(joint[i - 1], joint[i]) if i else pltpu.roll(joint[0], 4, 1)).astype(bf16)
+            last = joint[i].astype(bf16)
+            for half, pieces in enumerate(((first, moved[c, 4 * j + 1]), (moved[c, 4 * j + 2], last))):
+                turned = jnp.concatenate(pieces, axis=0).T
+                place = slice(256 * j + 128 * half, 256 * j + 128 * half + 128)
+                rest[32 * i : 32 * i + 32, :, place] = turned.reshape(32, 4, 128)
+
+    full_ahead.wait()
+    halo_prev[0] = dot(full_prev[...], ask[2]).astype(bf16)
+
+    def outer_west(q, carry):
+        @pl.when(q > 0)
+        def _():
+            from_prev(q).wait()
+
+        move(q, 0, gath[q, 0].astype(f32) + halo_prev[q].astype(f32), first_col)
+        return carry
+
     lax.fori_loop(0, CH, outer_west, 0)
 
 
-def share_kernel(moved, outside, parts, o_hbm, out, out_sem):
+def share_kernel(first_col, west_raw, outside, parts, rest, o_hbm, out, patch, out_sem):
     lane = iota((1, 128), 1)
+
+    def leave(i, src, dst):
+        copy = pltpu.make_async_copy(src, dst, out_sem.at[i])
+        copy.start()
+        return copy
+
+    copies = [leave(0, rest.at[1:96], o_hbm.at[33:128])]
 
     def after(a, b):
         return jnp.where(lane < 124, pltpu.roll(a, 124, 1), pltpu.roll(b, 124, 1))
@@ -369,28 +397,27 @@
     def before(a, b):
         return jnp.where(lane < 4, pltpu.roll(a, 4, 1), pltpu.roll(b, 4, 1))
 
-    leave = []
     for j in range(4):
-        mine = outside[j].astype(f32)
-        east = [mine] + [moved[c, 4 * j + 3].astype(f32) for c in range(4)]
-        west = [moved[c, 4 * j].astype(f32) for c in range(4)] + [mine]
-        now = [west[0]] + west[:4]
+        west = first_col[4 * j].astype(f32)
         joint = [
-            parts[0, i, j : j + 1] * east[i] + parts[1, i, j : j + 1] * after(now[i], west[i])
-            for i in range(5)
+            parts[0, 0, j : j + 1] * outside[j].astype(f32) + parts[1, 0, j : j + 1] * after(west, west),
+            parts[0, 1, j : j + 1] * first_col[4 * j + 3].astype(f32)
+            + parts[1, 1, j : j + 1] * after(west, west_raw[j].astype(f32)),
         ]
-        for c in range(4):
-            first = before(joint[c], joint[c + 1]).astype(bf16)
-            last = joint[c + 1].astype(bf16)
-            for half, pair in enumerate(((first, moved[c, 4 * j + 1]), (moved[c, 4 * j + 2], last))):
-                turned = jnp.concatenate(pair, axis=0).T
-                place = slice(256 * j + 128 * half, 256 * j + 128 * half + 128)
-                out[32 * c : 32 * c + 32, :, place] = turned.reshape(32, 4, 128)
-        place = slice(256 * j, 256 * j + 256)
-        copy = pltpu.make_async_copy(out.at[:, :, place], o_hbm.at[:, :, place], out_sem.at[j])
-        copy.start()
-        leave.append(copy)
-    for copy in leave:
+        first = before(joint[0], joint[1]).astype(bf16)
+        last = joint[1].astype(bf16)
+        for half, pieces in enumerate(((first, first_col[4 * j + 1]), (first_col[4 * j + 2], last))):
+            turned = jnp.concatenate(pieces, axis=0).T.reshape(32, 4, 128)
+            place = slice(256 * j + 128 * half, 256 * j + 128 * half + 128)
+            out[:, :, place] = turned
+        place = slice(256 * j, 256 * j + 128)
+        moved_over = pltpu.roll(turned[31].astype(f32), 64, 1)
+        patch[0, :, place] = jnp.where(lane < 64, moved_over, rest[0, :, place].astype(f32)).astype(bf16)
+        place = slice(256 * j + 128, 256 * j + 256)
+        patch[0, :, place] = rest[0, :, place]
+    copies.append(leave(1, out, o_hbm.at[0:32]))
+    copies.append(leave(2, patch, o_hbm.at[32:33]))
+    for copy in copies:
         copy.wait()
 
 
@@ -398,18 +425,20 @@
     peers_elem, peers_lev = mesh.shape["elem"], mesh.shape["lev"]
 
     def on_device(tracers, velocity, node_mass, source):
-        elements = tracers.shape[0]
+        elements, levels, columns = tracers.shape
         anywhere = pl.BlockSpec(memory_space=pl.ANY)
         vmem = pl.BlockSpec(memory_space=pltpu.VMEM)
         pieces = pl.pallas_call(
             functools.partial(kernel, peers_elem, peers_lev, elements * peers_elem),
             out_shape=(
-                pltpu.VMEM((4, 16, 64, 128), bf16),
+                pltpu.VMEM((16, 64, 128), bf16),
+                pltpu.VMEM((4, 64, 128), bf16),
                 pltpu.VMEM((4, 64, 128), bf16),
                 pltpu.VMEM((2, 5, 8, 128), f32),
+                pltpu.VMEM((elements - 32, levels, columns), bf16),
             ),
             in_specs=[anywhere] * 4,
-            out_specs=(vmem, vmem, vmem),
+            out_specs=(vmem,) * 5,
             scratch_shapes=[
                 pltpu.VMEM(tracers.shape, bf16),
                 pltpu.VMEM(velocity.shape, f32),
@@ -440,6 +469,7 @@
                 pltpu.VMEM((2, 512, 256), bf16),
                 pltpu.VMEM((16 * TQ, 256), bf16),
                 pltpu.VMEM((16 * TQ, 256), bf16),
+                pltpu.VMEM((4, 16, 64, 128), bf16),
                 pltpu.SemaphoreType.DMA((4,)),
                 pltpu.SemaphoreType.DMA((2, 2)),
                 pltpu.SemaphoreType.DMA((CH, 2)),
@@ -453,9 +483,13 @@
         return pl.pallas_call(
             share_kernel,
             out_shape=jax.ShapeDtypeStruct(tracers.shape, bf16),
-            in_specs=[vmem] * 3,
+            in_specs=[vmem] * 5,
             out_specs=anywhere,
-            scratch_shapes=[pltpu.VMEM(tracers.shape, bf16), pltpu.SemaphoreType.DMA((4,))],
+            scratch_shapes=[
+                pltpu.VMEM((32, levels, columns), bf16),
+                pltpu.VMEM((1, levels, columns), bf16),
+                pltpu.SemaphoreType.DMA((3,)),
+            ],
             compiler_params=pltpu.CompilerParams(vmem_limit_bytes=24 * 2**20),
             name="share",
         )(*pieces)

time: 34.9 us -> 34.2 us (0.980)
  Pallas kernels: 34.8 us -> 34 us
    pallas_call x1, Pallas kernels: 1.77 us -> 1.13 us  [on_device(): pl.pallas_call(share_kernel, out_shape=jax.ShapeDtypeStruct(tracers.shape...]
where the time goes in v5:
time: 34.2 us; the launch traced here: 34 us
  Pallas kernels  34 us (99%)
    pallas_call x1, Pallas kernels, on_device(): pl.pallas_call(functools.partial(kernel, peers_elem, peers_lev, elements...  32.9 us
    pallas_call x1, Pallas kernels, on_device(): pl.pallas_call(share_kernel, out_shape=jax.ShapeDtypeStruct(tracers.shape...  1.13 us

profile of v5, /device:TPU:6, one launch (start us, length us, event | category | flops | bytes accessed | tf_op | source)
XLA Modules:
  0.0 34.0 jit_solution(5407118365847212714)
XLA Ops:
  0.0 32.9 %transport.1 = (bf16[16,64,128]{2,1,0:T(8,128)(2,1)S(1)}, bf16[4,64,128]{2,1,0:T(8,128)(2,1)S(1)}, bf16[4,64,128]{2,1,0:T(8,128)(2,1)S(1)}, f32[2,5,8,128]{3,2,1,0:T(8,128)S(1)}, bf16[96,4,1024]{2,1,0:T(4,128)(2,1)S(1)}) custom-call(bf16[128,4,1024]{2,1,0:T(4,128)(2,1)} %t_hbm.1, f32[3,16,4,128]{3,2,1,0:T(4,128)} %v_hbm.1, f32[16,128]{1,0:T(8,128)} %mass_hbm.1, ...), custom_call_target="tpu_custom_call" | custom-call | tf_op jit(solution)/shard_map/transport/pallas_call | solution.py:431
  32.9 1.1 %share.1 = bf16[128,4,1024]{2,1,0:T(4,128)(2,1)} custom-call(bf16[16,64,128]{2,1,0:T(8,128)(2,1)S(1)} %get-tuple-element.10.first_col, bf16[4,64,128]{2,1,0:T(8,128)(2,1)S(1)} %get-tuple-element.11.west_raw, bf16[4,64,128]{2,1,0:T(8,128)(2,1)S(1)} %get-tuple-element.12.outside, f32[2,5,8,128]{3,2,1,0:T(8,128)S(1)} %get-tuple-element.13.parts, ...), custom_call_target="tpu_custom_call" | custom-call | tf_op jit(solution)/shard_map/share/pallas_call | solution.py:483
